TPU v7x, 32 devices: a whole 2x2x4 slice. The times are simulated.
32 devices in a mesh: seq: 8 (over z, x), head: 4 (over y, core).
Axes of the slice: x: 2, y: 2, z: 4, core: 2. Of those that a mesh axis runs over, the one named last changes fastest.
Arguments:
- queries: float32 [8192, 4096], P('seq', 'head'), may hold values from -6 to 6
- keys: float32 [8192, 4096], P('seq', 'head'), may hold values from -6 to 6
- values: float32 [8192, 4096], P('seq', 'head'), may hold values from -6 to 6
- out_grad: float32 [8192, 4096], P('seq', 'head'), may hold values from -6 to 6
- inputs: float32 [8192, 4096], P('seq', 'head'), may hold values from -20 to 20
- row_state: float32 [4, 4096], P('head', 'seq'), may hold values from 0.2 to 5
- col_state: float32 [8, 4096], P('seq', 'head'), may hold values from 0.2 to 5
Outputs:
- query_grad: float32 [8192, 4096], P('seq', 'head')
- key_grad: float32 [8192, 4096], P('seq', 'head')
- update: float32 [4096, 4096], P('seq', 'head')
- row_next: float32 [4, 4096], P('head', 'seq')
- col_next: float32 [8, 4096], P('seq', 'head')
All inputs are finite; a program needn't handle non-finite values.
Results may differ from a plain program's by a relative error of at most 0.0001.
Values sent between devices are 32-bit elements; how exact they have to be, the bound alone decides.
No kernel may reach another device: no remote copies, remote signals or barrier semaphores. Data moves between devices by JAX's collectives and lax.ppermute only.
A program may use at most 128 MiB of HBM per device.

v0:
```python
import functools
import jax
import jax.numpy as jnp
from jax import lax
from jax.experimental import pallas as pl
from jax.experimental.pallas import tpu as pltpu
from jax.sharding import PartitionSpec as P


HEAD_DIM = 128
MOMENT_EPS = 1e-06
DECAY = 0.9
F32 = jnp.float32
BF16 = jnp.bfloat16
AXES = ("seq", "head")
ALONE = 1
PIECES = ((2, 2), (2, 2))
SPLIT = (0, 1, 2, 3)
NN = (((1,), (0,)), ((), ()))
NT = (((1,), (1,)), ((), ()))
TN = (((0,), (0,)), ((), ()))


def split(x):
    hi = x.astype(BF16)
    return hi, (x - hi.astype(F32)).astype(BF16)


def times(a, b, dims):
    return lax.dot_general(a, b, dimension_numbers=dims, preferred_element_type=F32)


def mul_nn(a, b):
    wide = jnp.concatenate(b, axis=1)
    columns = b[0].shape[1]
    if a[0].shape[1] == HEAD_DIM:
        low = jnp.concatenate([b[0], jnp.zeros_like(b[0])], axis=1)
        out = times(jnp.concatenate(a, axis=1), jnp.concatenate([wide, low], axis=0), NN)
        return out[:, :columns] + out[:, columns:]
    out = times(a[0], wide, NN)
    return out[:, :columns] + (out[:, columns:] + times(a[1], b[0], NN))


def mul_nt(a, b):
    both = times(jnp.concatenate(a, axis=1), jnp.concatenate([b[0], b[0]], axis=1), NT)
    return both + times(a[0], b[1], NT)


def mul_tn(a, b):
    columns = b[0].shape[1]
    out = times(a[0], jnp.concatenate(b, axis=1), TN)
    return out[:, :columns] + (out[:, columns:] + times(a[1], b[0], TN))


def params(mib=24):
    return pltpu.CompilerParams(vmem_limit_bytes=mib * 2**20)


def cost(flops, nbytes):
    return pl.CostEstimate(flops=int(flops), bytes_accessed=int(nbytes), transcendentals=0)


def by_phase(phase, count):
    return lambda p, n: jnp.where(p == phase, n, jnp.where(p < phase, 0, count - 1))


def outer_body(low, scal, left, right, *outs):
    out = mul_tn(split(left[...]), split(right[...]))
    for jj in range(low):

        @pl.when(pl.program_id(0) == low - 1 - jj)
        def _():
            outs[jj][0] = out


def outer_sums(scal, left, right, low, chunks, begin, count):
    tokens = left.shape[0]
    spec = pl.BlockSpec(
        (tokens, HEAD_DIM), lambda p, n, s: (0, (s[1] ^ (low - 1 - p)) * chunks + begin + n)
    )

    def out_spec(jj):
        at = by_phase(low - 1 - jj, count)
        return pl.BlockSpec((1, HEAD_DIM, HEAD_DIM), lambda p, n, s: (at(p, n), 0, 0))

    return pl.pallas_call(
        functools.partial(outer_body, low),
        grid_spec=pltpu.PrefetchScalarGridSpec(
            num_scalar_prefetch=1,
            grid=(low, count),
            in_specs=[spec, spec],
            out_specs=[out_spec(jj) for jj in range(low)],
        ),
        out_shape=[jax.ShapeDtypeStruct((count, HEAD_DIM, HEAD_DIM), F32)] * low,
        compiler_params=params(),
        cost_estimate=cost(6 * low * count * tokens * HEAD_DIM**2, 8 * low * count * tokens * HEAD_DIM),
        name="outer_sums",
    )(scal, left, right)


def value_body(scale, blk, scal, q, k, g, mine, other, out):
    count = q.shape[0] // blk
    src = lax.broadcasted_iota(jnp.int32, (blk, blk), 0)
    tgt = lax.broadcasted_iota(jnp.int32, (blk, blk), 1)
    later = jnp.where(pl.program_id(0) == 0, mine[0], other[0])
    for n in reversed(range(count)):
        rows = pl.ds(n * blk, blk)
        qn, kn, gn = split(q[rows, :]), split(k[rows, :]), split(g[rows, :])
        scores = jnp.where(src <= tgt, mul_nt(kn, qn), 0.0)
        grad = mul_nn(split(scores), gn) + mul_nn(kn, split(later))
        out[0, :, rows] = (scale * grad).T
        if n:
            later = later + mul_tn(qn, gn)


def value_grads(scal, q, k, g, state, at, scale, low, chunks, a):
    tokens = q.shape[0]
    blk = min(256, tokens)
    spec = pl.BlockSpec((tokens, HEAD_DIM), lambda j, s: (0, (s[1] ^ j) * chunks + a))
    state_spec = pl.BlockSpec((1, HEAD_DIM, HEAD_DIM), lambda j, s: (at, 0, 0))
    return pl.pallas_call(
        functools.partial(value_body, scale, blk),
        grid_spec=pltpu.PrefetchScalarGridSpec(
            num_scalar_prefetch=1,
            grid=(low,),
            in_specs=[spec, spec, spec, state_spec, state_spec],
            out_specs=pl.BlockSpec((1, HEAD_DIM, tokens), lambda j, s: (s[1] ^ j, 0, 0)),
        ),
        out_shape=jax.ShapeDtypeStruct((low, HEAD_DIM, tokens), F32),
        compiler_params=params(),
        cost_estimate=cost(12 * low * tokens * blk * HEAD_DIM, 16 * low * tokens * HEAD_DIM),
        name="value_grads",
    )(scal, q, k, g, *state)


def query_key_body(scale, blk, scal, q, k, v, g, fwd, fwd_other, rev, rev_other, *refs):
    qg, kg = refs[-2:]
    count = q.shape[0] // blk
    here = pl.program_id(0) == 0
    tgt = lax.broadcasted_iota(jnp.int32, (blk, blk), 0)
    src = lax.broadcasted_iota(jnp.int32, (blk, blk), 1)
    before = [jnp.where(here, fwd[0], fwd_other[0])]
    for n in range(count - 1):
        rows = pl.ds(n * blk, blk)
        before.append(before[-1] + mul_tn(split(v[rows, :]), split(k[rows, :])))
    later = jnp.where(here, rev[0], rev_other[0])
    for n in reversed(range(count)):
        rows = pl.ds(n * blk, blk)
        qn, kn = split(q[rows, :]), split(k[rows, :])
        vn, gn = split(v[rows, :]), split(g[rows, :])
        scores = split(jnp.where(src <= tgt, mul_nt(gn, vn), 0.0))
        qg[rows, :] = scale * (mul_nn(scores, kn) + mul_nn(gn, split(before[n])))
        kg[rows, :] = scale * (mul_tn(scores, qn) + mul_nn(vn, split(later.T)))
        if n:
            later = later + mul_tn(qn, gn)


def query_key_grads(scal, q, k, v, g, fwd, rev, at, scale, low, chunks, a, count, filled):
    tokens, width = q.shape
    blk = min(256, tokens)
    spec = pl.BlockSpec((tokens, HEAD_DIM), lambda j, n, s: (0, (s[1] ^ j) * chunks + a + n))
    fwd_spec = pl.BlockSpec((1, HEAD_DIM, HEAD_DIM), lambda j, n, s: (a + n, 0, 0))
    rev_spec = pl.BlockSpec((1, HEAD_DIM, HEAD_DIM), lambda j, n, s: (at + n, 0, 0))
    kept = [pl.BlockSpec(memory_space=pl.ANY)] * len(filled)
    return pl.pallas_call(
        functools.partial(query_key_body, scale, blk),
        grid_spec=pltpu.PrefetchScalarGridSpec(
            num_scalar_prefetch=1,
            grid=(low, count),
            in_specs=[spec] * 4 + [fwd_spec] * 2 + [rev_spec] * 2 + kept,
            out_specs=[spec, spec],
        ),
        out_shape=[jax.ShapeDtypeStruct((tokens, width), F32)] * 2,
        input_output_aliases={9 + n: n for n in range(len(filled))},
        compiler_params=params(),
        cost_estimate=cost(30 * tokens * blk * low * count * HEAD_DIM, 24 * tokens * low * count * HEAD_DIM),
        name="query_key_grads",
    )(scal, q, k, v, g, *fwd, *rev, *filled)


def terms_body(*refs):
    pieces, (hi, lo) = refs[:-2], refs[-2:]
    at = 0
    for ref in pieces:
        cols = pl.ds(at, ref.shape[1])
        hi[:, cols], lo[:, cols] = split(ref[...])
        at += ref.shape[1]


def split_terms(pieces):
    tokens, width = pieces[0].shape[0], sum(x.shape[1] for x in pieces)
    blk = min(256, tokens)
    spec = pl.BlockSpec((blk, width), lambda n: (n, 0))
    return pl.pallas_call(
        terms_body,
        grid=(tokens // blk,),
        in_specs=[pl.BlockSpec((blk, x.shape[1]), lambda n: (n, 0)) for x in pieces],
        out_specs=[spec] * 2,
        out_shape=[jax.ShapeDtypeStruct((tokens, width), BF16)] * 2,
        compiler_params=params(),
        cost_estimate=cost(4 * tokens * width, 8 * tokens * width),
        name="split_terms",
    )(*pieces)


def rows_times(blocks, hi, lo):
    parts = [split(x) for x in blocks]
    high = jnp.concatenate([p[0] for p in parts], axis=0)
    both = jnp.concatenate([high] + [p[1] for p in parts], axis=0)
    wide = jnp.dot(both, hi, preferred_element_type=F32)
    rows = high.shape[0]
    return wide[:rows] + (wide[rows:] + jnp.dot(high, lo, preferred_element_type=F32))


def weight_body(ny, low, counts, scal, *refs):
    mine, other = refs[:ny], refs[ny : 2 * ny]
    own_hi, own_lo = refs[2 * ny : 2 * ny + 2]
    far, outs = refs[2 * ny + 2 : -low], refs[-low:]
    first = scal[0] == 1
    a, b = [x[0] for x in mine], [x[0] for x in other]
    if far:
        far_hi, far_lo, at = far[0][...], far[1][...], 0
        for c in range(1, len(counts)):
            at += counts[c - 1]
            later = pl.program_id(1) >= at
            far_hi = jnp.where(later, far[2 * c][...], far_hi)
            far_lo = jnp.where(later, far[2 * c + 1][...], far_lo)
        own_rows = [jnp.where(first, x, y) for x, y in zip(a, b)]
        far_rows = [jnp.where(first, y, x) for x, y in zip(a, b)]
        total = rows_times(own_rows, own_hi[...], own_lo[...]) + rows_times(far_rows, far_hi, far_lo)
        places = [(scal[2] ^ n,) for n in range(ny)]
    else:
        total = rows_times(a + b, own_hi[...], own_lo[...])
        places = [(1 - scal[0], scal[2] ^ n) for n in range(ny)]
        places += [(scal[0], scal[2] ^ n) for n in range(ny)]
    height = total.shape[0] // len(places)
    for jj in range(low):

        @pl.when(pl.program_id(0) == low - 1 - jj)
        def _():
            for n, place in enumerate(places):
                outs[jj][place] = total[n * height : (n + 1) * height]


def weight_parts(scal, mine, other, own, fars, offset, width):
    ny = len(mine)
    low, height, tokens = mine[0].shape
    widths = [x[0].shape[1] for x in fars] or [width]
    blk = 256 if all(x % 256 == 0 for x in widths + [offset]) else 128
    counts = [x // blk for x in widths]
    count, first = width // blk, offset // blk
    lead = (ny, height) if fars else (2, ny, height)
    grad_spec = pl.BlockSpec((1, height, tokens), lambda p, n, s: (s[1] ^ (low - 1 - p), 0, 0))
    own_spec = pl.BlockSpec((tokens, blk), lambda p, n, s: (0, n + first))

    def far_spec(c):
        begin = sum(counts[:c])
        return pl.BlockSpec((tokens, blk), lambda p, n, s: (0, jnp.clip(n - begin, 0, counts[c] - 1)))

    def out_spec(jj):
        col = by_phase(low - 1 - jj, count)
        zeros = (0,) * len(lead)
        return pl.BlockSpec(lead + (blk,), lambda p, n, s: zeros + (col(p, n),))

    return pl.pallas_call(
        functools.partial(weight_body, ny, low, counts),
        grid_spec=pltpu.PrefetchScalarGridSpec(
            num_scalar_prefetch=1,
            grid=(low, count),
            in_specs=[grad_spec] * (2 * ny)
            + [own_spec] * 2
            + [far_spec(c) for c in range(len(fars)) for _ in range(2)],
            out_specs=[out_spec(jj) for jj in range(low)],
        ),
        out_shape=[jax.ShapeDtypeStruct(lead + (width,), F32)] * low,
        compiler_params=params(),
        cost_estimate=cost(
            12 * ny * low * height * tokens * width,
            8 * ny * low * height * tokens + 8 * tokens * width + 8 * ny * height * width,
        ),
        name="weight_parts",
    )(scal, *mine, *other, *own, *[x for pair in fars for x in pair])


def update_body(scale, counts, row_state, col_state, *refs):
    parts, (update, row_next, col_next) = list(refs[:-3]), refs[-3:]
    height = parts[0].shape[-2]
    rows, columns = update.shape
    row_cols = []
    total = jnp.zeros((1, 1), F32)
    col_next[...] = jnp.zeros_like(col_next)
    for a, cells in enumerate(counts):
        at = pl.ds(a * height, height)
        row_sum, begin = jnp.zeros((height, 1), F32), 0
        for count in cells:
            cols = pl.ds(begin, parts[0].shape[-1])
            begin += parts[0].shape[-1]
            block = parts.pop(0)[0]
            for _ in range(count - 1):
                block = block + parts.pop(0)[0]
            block = block * scale
            update[at, cols] = block
            squares = block * block
            row_sum = row_sum + jnp.sum(squares, axis=1, keepdims=True)
            col_next[:, cols] += jnp.sum(squares, axis=0, keepdims=True)
        mean = row_sum * (1.0 / columns) + MOMENT_EPS
        lanes = jnp.broadcast_to(mean, (height, height)).T[:1]
        nxt = DECAY * row_state[:, at] + (1.0 - DECAY) * lanes
        row_next[:, at] = nxt
        total = total + jnp.sum(nxt, axis=1, keepdims=True)
        row_cols.append(jnp.broadcast_to(nxt, (height, height)).T[:, :1])
    average = total * (1.0 / rows)
    nxt = DECAY * col_state[...] + (1.0 - DECAY) * (col_next[...] * (1.0 / rows) + MOMENT_EPS)
    col_next[...] = nxt
    for a in range(len(counts)):
        at = pl.ds(a * height, height)
        update[at, :] = update[at, :] / jnp.sqrt(row_cols[a] * nxt / average)


def update_block(parts, row_state, col_state, scale):
    chunks = len(parts)
    counts = tuple(tuple(len(cell) for cell in row) for row in parts)
    flat = [x for row in parts for cell in row for x in cell]
    height = flat[0].shape[-2]
    cell = lambda x: pl.BlockSpec((1,) + x.shape[-2:], lambda n: (0, 0, 0))
    full = lambda x: pl.BlockSpec(x.shape, lambda n: (0, 0))
    shape = (chunks * height, col_state.shape[1])
    out_shape = [
        jax.ShapeDtypeStruct(shape, F32),
        jax.ShapeDtypeStruct(row_state.shape, F32),
        jax.ShapeDtypeStruct(col_state.shape, F32),
    ]
    return pl.pallas_call(
        functools.partial(update_body, scale, counts),
        grid=(1,),
        in_specs=[full(row_state), full(col_state)] + [cell(x) for x in flat],
        out_specs=[full(x) for x in out_shape],
        out_shape=out_shape,
        compiler_params=params(),
        cost_estimate=cost(20 * shape[0] * shape[1], 16 * shape[0] * shape[1]),
        name="update_block",
    )(row_state, col_state, *flat)


def shards(queries, keys, values, out_grad, inputs, row_state, col_state):
    tokens, width = queries.shape
    n_seq, n_head = lax.axis_size("seq"), lax.axis_size("head")
    heads = width // HEAD_DIM
    low = n_seq // n_head
    ny = n_head // 2
    chunks = heads // low
    scale = 1.0 / float(HEAD_DIM * tokens * n_seq) ** 0.5
    weight_scale = 1.0 / float(tokens * n_seq) ** 0.5
    assert low == 2 and chunks > 1

    def permute(x, go):
        pairs = []
        for s in range(n_seq):
            for h in range(n_head):
                to = go(s, h)
                if to is not None:
                    pairs.append((s * n_head + h, to[0] * n_head + to[1]))
        return lax.ppermute(x, AXES, pairs)

    def over_seq(x, bit):
        return permute(x, lambda s, h: (s ^ bit, h))

    def over_head(x, bit):
        return permute(x, lambda s, h: (s, h ^ bit))

    seq, head = lax.axis_index("seq"), lax.axis_index("head")
    plane = (seq // low) & 1
    first = plane == (head & 1)
    part = seq % low
    scal = jnp.stack([first.astype(jnp.int32), part, (head // 2) ^ (seq // (2 * low))]).astype(jnp.int32)

    def scan_states(sums, reverse):
        keep, send = sums
        got = over_seq(send, 1)
        total, enter, bit = keep + got, jnp.zeros_like(keep), low
        while bit < n_seq:
            came = over_seq(total, bit)
            take = ((seq & bit) == 0) if reverse else ((seq & bit) != 0)
            enter = enter + jnp.where(take, came, 0.0)
            bit *= 2
            if bit < n_seq:
                total = total + came
        last = 0 if reverse else 1
        mine = enter + jnp.where(part == last, got, 0.0)
        out = enter + jnp.where(part == last, 0.0, keep)
        return mine, over_seq(out, 1)

    sums = outer_sums(scal, queries, out_grad, low, chunks, 0, 1)
    rest = outer_sums(scal, queries, out_grad, low, chunks, 1, chunks - 1)
    own_terms = split_terms([inputs])
    rev0 = scan_states(sums, True)
    rev1 = scan_states(rest, True)
    fwd = scan_states(outer_sums(scal, values, keys, low, chunks, 0, chunks), False)

    eighth, at, far_terms = inputs.shape[1] // 8, 0, []
    for sizes in PIECES:
        pieces = []
        for size in sizes:
            piece = inputs[:, at * eighth : (at + size) * eighth]
            pieces.append(over_seq(piece, low))
            at = at + size
        far_terms.append(split_terms(pieces))

    def state_of(a):
        return (rev0, 0) if a == 0 else (rev1, a - 1)

    gathered = []
    for a in range(chunks):
        grads = value_grads(scal, queries, keys, out_grad, *state_of(a), scale, low, chunks, a)
        if a >= ALONE:
            got = permute(
                grads, lambda s, h: None if ((s // low) & 1) == (h & 1) else (s ^ low, h ^ 1)
            )
            grads = jnp.where(first, grads, got)
        mine, other, bit = [grads], [over_head(grads, 1)], 1
        while bit < ny:
            more = [over_head(x, 2 * bit) for x in mine]
            mine, other = mine + more, other + [over_head(x, 1) for x in more]
            bit *= 2
        gathered.append((mine, other))

    def reduced(added, bit):
        count = added[0].shape[0]
        while count > 1:
            count //= 2
            both = functools.reduce(jnp.add, added)
            added = [both[:count], over_seq(both[count:], bit * count)]
        return added

    cells = []
    for a in range(chunks):
        row, offset = [], 0
        groups = [[x] for x in far_terms] if a in SPLIT else [far_terms]
        for fars in groups:
            size = sum(x[0].shape[1] for x in fars)
            keep, send = weight_parts(
                scal, *gathered[a], own_terms,
                fars if a >= ALONE else [], offset, size,
            )
            offset += size
            parts = [keep, over_seq(send, 1)]
            if a < ALONE:
                parts = [x[0] for x in reduced(parts, low)]
            row.append(reduced(parts, 2 * low))
        cells.append(row)

    grads = ()
    for begin, count in ((0, 1), (1, chunks - 1)):
        rev, at = state_of(begin)
        grads = query_key_grads(
            scal, queries, keys, values, out_grad,
            fwd, rev, at, scale, low, chunks, begin, count, grads,
        )
    update, row_next, col_next = update_block(cells, row_state, col_state, weight_scale)
    return (*grads, update, row_next, col_next)


def solution(mesh):
    tok, rows = P("seq", "head"), P("head", "seq")

    return jax.shard_map(
        shards,
        mesh=mesh,
        in_specs=(tok, tok, tok, tok, tok, rows, tok),
        out_specs=(tok, tok, tok, rows, tok),
        check_vma=False,
    )
```

profile of v0, /device:TPU:0, one launch (start us, length us, event | category | flops | bytes accessed | tf_op | source)
XLA Modules:
  0.0 370.5 jit_solution(13334680249774036787)
XLA Ops:
  0.8 2.2 copy-done
  2.9 2.2 copy-done.4
  6.7 3.0 collective-permute-start.8
  9.8 2.2 collective-permute-done.8
  12.0 2.2 collective-permute-start.9
  14.2 2.2 collective-permute-done.9
  16.5 3.1 collective-permute-start.10
  19.6 2.2 collective-permute-done.10
  21.8 1.9 collective-permute-start.11
  23.7 2.4 collective-permute-done.11.rev_other.other
  26.2 2.2 copy-done.1
  28.4 2.2 copy-done.5
  30.5 2.2 copy-done.8
  32.7 4.0 %value_grads.4.refs_0_ = f32[2,128,1024]{2,1,0:T(8,128)S(1)} custom-call(s32[3]{0:T(128)S(1)} %pad_add_fusion.scal, f32[1024,1024]{1,0:T(8,128)S(1)} %copy-done.1, f32[1024,1024]{1,0:T(8,128)S(1)} %copy-done.8, f32[1024,1024]{1,0:T(8,128)S(1)} %copy-done.5, f32[1,128,128]{2,1,0:T(8,128)S(1)} %get-tuple-element.100.rev.mine, ...), custom_call_target="tpu_custom_call" | custom-call | flops 805306368 | bytes 4194304 | tf_op jit(solution)/shard_map/value_grads/pallas_call | solution.py:121
  38.0 1.9 collective-permute-start.12
  39.8 3.7 outer_sums.4
  45.1 4.7 %outer_sums.3 = (f32[4,128,128]{2,1,0:T(8,128)S(1)}, f32[4,128,128]{2,1,0:T(8,128)S(1)}) custom-call(s32[3]{0:T(128)S(1)} %pad_add_fusion.scal, f32[1024,1024]{1,0:T(8,128)S(1)} %copy-done.11, f32[1024,1024]{1,0:T(8,128)S(1)} %copy-done.9), custom_call_target="tpu_custom_call" | custom-call | flops 805306368 | bytes 8388608 | tf_op jit(solution)/shard_map/outer_sums/pallas_call | solution.py:86
  52.7 3.6 collective-permute-done
  58.0 5.2 %collective-permute-start.6 = (f32[3,128,128]{2,1,0:T(8,128)S(1)}, f32[3,128,128]{2,1,0:T(8,128)S(1)}, u32[]{:S(2)}, u32[]{:S(2)}) collective-permute-start(f32[3,128,128]{2,1,0:T(8,128)S(1)} %add.91), channel_id=1, source_target_pairs={{0,16},{1,17},{2,18},{3,19},{4,20},{5,21},{6,22},{7,23},{8,24},{9,... | collective-permute-start | bytes 589832 | tf_op jit(solution)/shard_map/ppermute | solution.py:363
  64.5 2.6 collective-permute-start.29
  69.2 3.1 collective-permute-start.7
  72.2 23.6 %collective-permute-done.2 = f32[4,128,128]{2,1,0:T(8,128)S(1)} collective-permute-done((f32[4,128,128]{2,1,0:T(8,128)S(1)}, f32[4,128,128]{2,1,0:T(8,128)S(1)}, u32[]{:S(2)}, u32[]{:S(2)}) %collective-permute-start.2) | collective-permute-done | bytes 262176 | tf_op jit(solution)/shard_map/ppermute | solution.py:363
  95.9 1.7 collective-permute-start.30
  97.9 4.0 %value_grads.7 = f32[2,128,1024]{2,1,0:T(8,128)S(1)} custom-call(s32[3]{0:T(128)S(1)} %pad_add_fusion.scal, f32[1024,1024]{1,0:T(8,128)S(1)} %copy-done.2, f32[1024,1024]{1,0:T(8,128)S(1)} %copy-done.9, f32[1024,1024]{1,0:T(8,128)S(1)} %copy-done.6, f32[3,128,128]{2,1,0:T(8,128)S(1)} %get-tuple-element.98.rev.mine, ...), custom_call_target="tpu_custom_call" | custom-call | flops 805306368 | bytes 4194304 | tf_op jit(solution)/shard_map/value_grads/pallas_call | solution.py:121
  103.3 4.0 %value_grads.6 = f32[2,128,1024]{2,1,0:T(8,128)S(1)} custom-call(s32[3]{0:T(128)S(1)} %pad_add_fusion.scal, f32[1024,1024]{1,0:T(8,128)S(1)} %copy-done.2, f32[1024,1024]{1,0:T(8,128)S(1)} %copy-done.9, f32[1024,1024]{1,0:T(8,128)S(1)} %copy-done.6, f32[3,128,128]{2,1,0:T(8,128)S(1)} %get-tuple-element.98.rev.mine, ...), custom_call_target="tpu_custom_call" | custom-call | flops 805306368 | bytes 4194304 | tf_op jit(solution)/shard_map/value_grads/pallas_call | solution.py:121
  108.2 5.5 %weight_parts.9 = (f32[2,2,128,512]{3,2,1,0:T(8,128)S(1)}, f32[2,2,128,512]{3,2,1,0:T(8,128)S(1)}) custom-call(s32[3]{0:T(128)S(1)} %pad_add_fusion.scal, f32[2,128,1024]{2,1,0:T(8,128)S(1)} %value_grads.4.refs_0_, f32[2,128,1024]{2,1,0:T(8,128)S(1)} %collective-permute-done.12.refs_1_, f32[2,128,1024]{2,1,0:T(8,128)S(1)} %collective-permute-done.13.refs_2_, ...), custom_call_target="tpu_custom_call" | custom-call | flops 3221225472 | bytes 9437184 | tf_op jit(solution)/shard_map/weight_parts/pallas_call | solution.py:265
  113.8 2.0 collective-permute-start.18
  115.8 6.3 %weight_parts.8 = (f32[2,2,128,512]{3,2,1,0:T(8,128)S(1)}, f32[2,2,128,512]{3,2,1,0:T(8,128)}) custom-call(s32[3]{0:T(128)S(1)} %pad_add_fusion.scal, f32[2,128,1024]{2,1,0:T(8,128)S(1)} %value_grads.4.refs_0_, f32[2,128,1024]{2,1,0:T(8,128)S(1)} %collective-permute-done.12.refs_1_, f32[2,128,1024]{2,1,0:T(8,128)S(1)} %collective-permute-done.13.refs_2_, ...), custom_call_target="tpu_custom_call" | custom-call | flops 3221225472 | bytes 9437184 | tf_op jit(solution)/shard_map/weight_parts/pallas_call | solution.py:265
  123.0 1.8 collective-permute-start.15
  124.8 18.8 %collective-permute-done.25.refs_0_ = f32[1024,256]{1,0:T(8,128)S(1)} collective-permute-done((f32[1024,256]{1,0:T(8,128)S(1)}, f32[1024,256]{1,0:T(8,128)S(1)}, u32[]{:S(2)}, u32[]{:S(2)}) %collective-permute-start.25) | collective-permute-done | bytes 1048608 | tf_op jit(solution)/shard_map/ppermute | solution.py:363
  143.6 2.5 collective-permute-start.26
  146.1 4.0 %value_grads.5 = f32[2,128,1024]{2,1,0:T(8,128)S(1)} custom-call(s32[3]{0:T(128)S(1)} %pad_add_fusion.scal, f32[1024,1024]{1,0:T(8,128)S(1)} %copy-done.2, f32[1024,1024]{1,0:T(8,128)S(1)} %copy-done.9, f32[1024,1024]{1,0:T(8,128)S(1)} %copy-done.6, f32[3,128,128]{2,1,0:T(8,128)S(1)} %get-tuple-element.98.rev.mine, ...), custom_call_target="tpu_custom_call" | custom-call | flops 805306368 | bytes 4194304 | tf_op jit(solution)/shard_map/value_grads/pallas_call | solution.py:121
  159.1 24.9 %collective-permute-start.19 = (f32[1,2,128,512]{3,2,1,0:T(8,128)S(1)}, f32[1,2,128,512]{3,2,1,0:T(8,128)S(1)}, u32[]{:S(2)}, u32[]{:S(2)}) collective-permute-start(f32[1,2,128,512]{3,2,1,0:T(8,128)S(1)} %slice.117), channel_id=1, source_target_pairs={{0,8},{1,9},{2,10},{3,11},{4,12},{5,13},{6,14},{7,15},{8,0},{9,1},... | collective-permute-start | bytes 1572872 | tf_op jit(solution)/shard_map/ppermute | solution.py:363
  185.6 5.6 %collective-permute-done.26.refs_1_ = f32[1024,256]{1,0:T(8,128)} collective-permute-done((f32[1024,256]{1,0:T(8,128)}, f32[1024,256]{1,0:T(8,128)}, u32[]{:S(2)}, u32[]{:S(2)}) %collective-permute-start.26) | collective-permute-done | bytes 1048608 | tf_op jit(solution)/shard_map/ppermute | solution.py:363
  191.1 1.9 collective-permute-start.3
  193.1 13.2 %collective-permute-start.16 = (f32[1,2,128,512]{3,2,1,0:T(8,128)S(1)}, f32[1,2,128,512]{3,2,1,0:T(8,128)S(1)}, u32[]{:S(2)}, u32[]{:S(2)}) collective-permute-start(f32[1,2,128,512]{3,2,1,0:T(8,128)S(1)} %slice.113), channel_id=1, source_target_pairs={{0,8},{1,9},{2,10},{3,11},{4,12},{5,13},{6,14},{7,15},{8,0},{9,1},... | collective-permute-start | bytes 1572872 | tf_op jit(solution)/shard_map/ppermute | solution.py:363
  207.1 6.5 %collective-permute-done.19 = f32[1,2,128,512]{3,2,1,0:T(8,128)S(1)} collective-permute-done((f32[1,2,128,512]{3,2,1,0:T(8,128)S(1)}, f32[1,2,128,512]{3,2,1,0:T(8,128)S(1)}, u32[]{:S(2)}, u32[]{:S(2)}) %collective-permute-start.19) | collective-permute-done | bytes 524320 | tf_op jit(solution)/shard_map/ppermute | solution.py:363
  213.6 2.2 copy-done.12
  215.8 6.3 %query_key_grads.2 = (f32[1024,1024]{1,0:T(8,128)}, f32[1024,1024]{1,0:T(8,128)}) custom-call(s32[3]{0:T(128)S(1)} %pad_add_fusion.scal, f32[1024,1024]{1,0:T(8,128)S(1)} %copy-done.3, f32[1024,1024]{1,0:T(8,128)S(1)} %copy-done.10, f32[1024,1024]{1,0:T(8,128)S(1)} %copy-done.12, f32[1024,1024]{1,0:T(8,128)S(1)} %copy-done.7, ...), custom_call_target="tpu_custom_call" | custom-call | flops 2013265920 | bytes 6291456 | tf_op jit(solution)/shard_map/query_key_grads/pallas_call | solution.py:165
  222.5 2.5 split_terms.4
  226.5 5.6 %collective-permute-done.22.refs_1_ = f32[2,128,1024]{2,1,0:T(8,128)S(1)} collective-permute-done((f32[2,128,1024]{2,1,0:T(8,128)S(1)}, f32[2,128,1024]{2,1,0:T(8,128)S(1)}, u32[]{:S(2)}, u32[]{:S(2)}) %collective-permute-start.22) | collective-permute-done | bytes 1048608 | tf_op jit(solution)/shard_map/ppermute | solution.py:363
  232.1 2.7 collective-permute-start.20
  234.8 7.0 %weight_parts.15 = (f32[2,128,512]{2,1,0:T(8,128)S(1)}, f32[2,128,512]{2,1,0:T(8,128)S(1)}) custom-call(s32[3]{0:T(128)S(1)} %pad_add_fusion.scal, f32[2,128,1024]{2,1,0:T(8,128)} %broadcast_select_fusion.refs_0_, f32[2,128,1024]{2,1,0:T(8,128)} %collective-permute-done.42.refs_1_, f32[2,128,1024]{2,1,0:T(8,128)S(1)} %collective-permute-done.43.refs_2_, ...), custom_call_target="tpu_custom_call" | custom-call | flops 3221225472 | bytes 9437184 | tf_op jit(solution)/shard_map/weight_parts/pallas_call | solution.py:265
  241.8 7.0 %weight_parts.14 = (f32[2,128,512]{2,1,0:T(8,128)S(1)}, f32[2,128,512]{2,1,0:T(8,128)S(1)}) custom-call(s32[3]{0:T(128)S(1)} %pad_add_fusion.scal, f32[2,128,1024]{2,1,0:T(8,128)} %broadcast_select_fusion.refs_0_, f32[2,128,1024]{2,1,0:T(8,128)} %collective-permute-done.42.refs_1_, f32[2,128,1024]{2,1,0:T(8,128)S(1)} %collective-permute-done.43.refs_2_, ...), custom_call_target="tpu_custom_call" | custom-call | flops 3221225472 | bytes 9437184 | tf_op jit(solution)/shard_map/weight_parts/pallas_call | solution.py:265
  248.9 2.0 collective-permute-start.47
  251.0 7.0 %weight_parts.13 = (f32[2,128,512]{2,1,0:T(8,128)S(1)}, f32[2,128,512]{2,1,0:T(8,128)S(1)}) custom-call(s32[3]{0:T(128)S(1)} %pad_add_fusion.scal, f32[2,128,1024]{2,1,0:T(8,128)} %broadcast_select_fusion.1.refs_0_, f32[2,128,1024]{2,1,0:T(8,128)} %collective-permute-done.34.refs_1_, f32[2,128,1024]{2,1,0:T(8,128)S(1)} %collective-permute-done.35.refs_2_, ...), custom_call_target="tpu_custom_call" | custom-call | flops 3221225472 | bytes 9437184 | tf_op jit(solution)/shard_map/weight_parts/pallas_call | solution.py:265
  258.0 7.0 %weight_parts.12 = (f32[2,128,512]{2,1,0:T(8,128)S(1)}, f32[2,128,512]{2,1,0:T(8,128)S(1)}) custom-call(s32[3]{0:T(128)S(1)} %pad_add_fusion.scal, f32[2,128,1024]{2,1,0:T(8,128)} %broadcast_select_fusion.1.refs_0_, f32[2,128,1024]{2,1,0:T(8,128)} %collective-permute-done.34.refs_1_, f32[2,128,1024]{2,1,0:T(8,128)S(1)} %collective-permute-done.35.refs_2_, ...), custom_call_target="tpu_custom_call" | custom-call | flops 3221225472 | bytes 9437184 | tf_op jit(solution)/shard_map/weight_parts/pallas_call | solution.py:265
  265.0 2.0 collective-permute-start.39
  267.1 6.0 %weight_parts.11 = (f32[2,128,512]{2,1,0:T(8,128)S(1)}, f32[2,128,512]{2,1,0:T(8,128)S(1)}) custom-call(s32[3]{0:T(128)S(1)} %pad_add_fusion.scal, f32[2,128,1024]{2,1,0:T(8,128)S(1)} %broadcast_select_fusion.2.refs_0_, f32[2,128,1024]{2,1,0:T(8,128)S(1)} %collective-permute-done.22.refs_1_, f32[2,128,1024]{2,1,0:T(8,128)S(1)} %collective-permute-done.23.refs_2_, ...), custom_call_target="tpu_custom_call" | custom-call | flops 3221225472 | bytes 9437184 | tf_op jit(solution)/shard_map/weight_parts/pallas_call | solution.py:265
  273.1 6.2 %weight_parts.10 = (f32[2,128,512]{2,1,0:T(8,128)S(1)}, f32[2,128,512]{2,1,0:T(8,128)S(1)}) custom-call(s32[3]{0:T(128)S(1)} %pad_add_fusion.scal, f32[2,128,1024]{2,1,0:T(8,128)S(1)} %broadcast_select_fusion.2.refs_0_, f32[2,128,1024]{2,1,0:T(8,128)S(1)} %collective-permute-done.22.refs_1_, f32[2,128,1024]{2,1,0:T(8,128)S(1)} %collective-permute-done.23.refs_2_, ...), custom_call_target="tpu_custom_call" | custom-call | flops 3221225472 | bytes 9437184 | tf_op jit(solution)/shard_map/weight_parts/pallas_call | solution.py:265
  279.3 2.0 collective-permute-start.31
  281.8 4.4 %collective-permute-done.39 = f32[2,128,512]{2,1,0:T(8,128)S(1)} collective-permute-done((f32[2,128,512]{2,1,0:T(8,128)S(1)}, f32[2,128,512]{2,1,0:T(8,128)S(1)}, u32[]{:S(2)}, u32[]{:S(2)}) %collective-permute-start.39) | collective-permute-done | bytes 524320 | tf_op jit(solution)/shard_map/ppermute | solution.py:363
  286.2 1.9 collective-permute-start.27
  288.3 9.1 %collective-permute-done.37 = f32[2,128,512]{2,1,0:T(8,128)S(1)} collective-permute-done((f32[2,128,512]{2,1,0:T(8,128)S(1)}, f32[2,128,512]{2,1,0:T(8,128)S(1)}, u32[]{:S(2)}, u32[]{:S(2)}) %collective-permute-start.37) | collective-permute-done | bytes 524320 | tf_op jit(solution)/shard_map/ppermute | solution.py:363
  297.7 10.9 %collective-permute-done.31 = f32[2,128,512]{2,1,0:T(8,128)S(1)} collective-permute-done((f32[2,128,512]{2,1,0:T(8,128)S(1)}, f32[2,128,512]{2,1,0:T(8,128)S(1)}, u32[]{:S(2)}, u32[]{:S(2)}) %collective-permute-start.31) | collective-permute-done | bytes 524320 | tf_op jit(solution)/shard_map/ppermute | solution.py:363
  309.1 10.3 %collective-permute-done.27 = f32[2,128,512]{2,1,0:T(8,128)S(1)} collective-permute-done((f32[2,128,512]{2,1,0:T(8,128)S(1)}, f32[2,128,512]{2,1,0:T(8,128)S(1)}, u32[]{:S(2)}, u32[]{:S(2)}) %collective-permute-start.27) | collective-permute-done | bytes 524320 | tf_op jit(solution)/shard_map/ppermute | solution.py:363
  319.8 2.7 collective-permute-start.38
  322.8 2.6 collective-permute-start.28
  325.4 15.6 %query_key_grads.3 = (f32[1024,1024]{1,0:T(8,128)}, f32[1024,1024]{1,0:T(8,128)}) custom-call(s32[3]{0:T(128)S(1)} %pad_add_fusion.scal, f32[1024,1024]{1,0:T(8,128)S(1)} %copy-done.3, f32[1024,1024]{1,0:T(8,128)S(1)} %copy-done.10, f32[1024,1024]{1,0:T(8,128)S(1)} %copy-done.13, ...), custom_call_target="tpu_custom_call", output_to_operand_aliasing={{0}: (9, {}), {1}: (10, {})} | custom-call | flops 6039797760 | bytes 18874368 | tf_op jit(solution)/shard_map/query_key_grads/pallas_call | solution.py:165
  341.0 9.9 %collective-permute-done.40.refs_11_ = f32[1,128,512]{2,1,0:T(8,128)S(1)} collective-permute-done((f32[1,128,512]{2,1,0:T(8,128)S(1)}, f32[1,128,512]{2,1,0:T(8,128)S(1)}, u32[]{:S(2)}, u32[]{:S(2)}) %collective-permute-start.40) | collective-permute-done | bytes 262176 | tf_op jit(solution)/shard_map/ppermute | solution.py:363
  350.9 5.6 %collective-permute-done.38.refs_9_ = f32[1,128,512]{2,1,0:T(8,128)S(1)} collective-permute-done((f32[1,128,512]{2,1,0:T(8,128)S(1)}, f32[1,128,512]{2,1,0:T(8,128)S(1)}, u32[]{:S(2)}, u32[]{:S(2)}) %collective-permute-start.38) | collective-permute-done | bytes 262176 | tf_op jit(solution)/shard_map/ppermute | solution.py:363
  356.5 5.6 %collective-permute-done.32.refs_7_ = f32[1,128,512]{2,1,0:T(8,128)S(1)} collective-permute-done((f32[1,128,512]{2,1,0:T(8,128)S(1)}, f32[1,128,512]{2,1,0:T(8,128)S(1)}, u32[]{:S(2)}, u32[]{:S(2)}) %collective-permute-start.32) | collective-permute-done | bytes 262176 | tf_op jit(solution)/shard_map/ppermute | solution.py:363
  362.1 5.2 %collective-permute-done.28.refs_5_ = f32[1,128,512]{2,1,0:T(8,128)S(1)} collective-permute-done((f32[1,128,512]{2,1,0:T(8,128)S(1)}, f32[1,128,512]{2,1,0:T(8,128)S(1)}, u32[]{:S(2)}, u32[]{:S(2)}) %collective-permute-start.28) | collective-permute-done | bytes 262176 | tf_op jit(solution)/shard_map/ppermute | solution.py:363
  367.3 3.1 update_block.1
  (163 shorter events, 31.5 us)
Async XLA Ops:
  6.7 5.3 %collective-permute-start.8 = (f32[1,128,128]{2,1,0:T(8,128)S(1)}, f32[1,128,128]{2,1,0:T(8,128)S(1)}, u32[]{:S(2)}, u32[]{:S(2)}) collective-permute-start(f32[1,128,128]{2,1,0:T(8,128)S(1)} %get-tuple-element.45), channel_id=1, source_target_pairs={{0,4},{1,5},{2,6},{3,7},{4,0},{5,1},{6,2},{7,3},{8,12},{9,13},{10,... | collective-permute-start | bytes 196616 | tf_op jit(solution)/shard_map/ppermute | solution.py:363
  12.0 4.4 %collective-permute-start.9 = (f32[1,128,128]{2,1,0:T(8,128)S(1)}, f32[1,128,128]{2,1,0:T(8,128)S(1)}, u32[]{:S(2)}, u32[]{:S(2)}) collective-permute-start(f32[1,128,128]{2,1,0:T(8,128)S(1)} %add.95), channel_id=1, source_target_pairs={{0,8},{1,9},{2,10},{3,11},{4,12},{5,13},{6,14},{7,15},{8,0},{9,1},... | collective-permute-start | bytes 196616 | tf_op jit(solution)/shard_map/ppermute | solution.py:363
  16.5 5.3 %collective-permute-start.10 = (f32[1,128,128]{2,1,0:T(8,128)S(1)}, f32[1,128,128]{2,1,0:T(8,128)S(1)}, u32[]{:S(2)}, u32[]{:S(2)}) collective-permute-start(f32[1,128,128]{2,1,0:T(8,128)S(1)} %add.96), channel_id=1, source_target_pairs={{0,16},{1,17},{2,18},{3,19},{4,20},{5,21},{6,22},{7,23},{8,24},{9,... | collective-permute-start | bytes 196616 | tf_op jit(solution)/shard_map/ppermute | solution.py:363
  21.8 4.3 %collective-permute-start.11 = (f32[1,128,128]{2,1,0:T(8,128)S(1)}, f32[1,128,128]{2,1,0:T(8,128)S(1)}, u32[]{:S(2)}, u32[]{:S(2)}) collective-permute-start(f32[1,128,128]{2,1,0:T(8,128)S(1)} %get-tuple-element.99), channel_id=1, source_target_pairs={{0,4},{1,5},{2,6},{3,7},{4,0},{5,1},{6,2},{7,3},{8,12},{9,13},{10,... | collective-permute-start | bytes 196616 | tf_op jit(solution)/shard_map/ppermute | solution.py:363
  38.0 25.2 %collective-permute-start.12 = (f32[2,128,1024]{2,1,0:T(8,128)S(1)}, f32[2,128,1024]{2,1,0:T(8,128)S(1)}, u32[]{:S(2)}, u32[]{:S(2)}) collective-permute-start(f32[2,128,1024]{2,1,0:T(8,128)S(1)} %value_grads.4.refs_0_), channel_id=1, source_target_pairs={{0,2},{1,3},{2,0},{3,1},{4,6},{5,7},{6,4},{7,5},{8,10},{9,11},{10,... | collective-permute-start | bytes 3145736 | tf_op jit(solution)/shard_map/ppermute | solution.py:363
  43.5 19.6 %copy-start.14 = (f32[1024,1024]{1,0:T(8,128)S(1)}, f32[1024,1024]{1,0:T(8,128)}, u32[]{:S(2)}) copy-start(f32[1024,1024]{1,0:T(8,128)} %refs_0_.1) | copy-start | bytes 12582916
  43.6 7.6 %collective-permute-start.4 = (f32[3,128,128]{2,1,0:T(8,128)S(1)}, f32[3,128,128]{2,1,0:T(8,128)S(1)}, u32[]{:S(2)}, u32[]{:S(2)}) collective-permute-start(f32[3,128,128]{2,1,0:T(8,128)S(1)} %get-tuple-element.43), channel_id=1, source_target_pairs={{0,4},{1,5},{2,6},{3,7},{4,0},{5,1},{6,2},{7,3},{8,12},{9,13},{10,... | collective-permute-start | bytes 589832 | tf_op jit(solution)/shard_map/ppermute | solution.py:363
  49.8 14.7 %copy-start.15 = (f32[4,128,128]{2,1,0:T(8,128)}, f32[4,128,128]{2,1,0:T(8,128)S(1)}, u32[]{:S(2)}) copy-start(f32[4,128,128]{2,1,0:T(8,128)S(1)} %get-tuple-element.40) | copy-start | bytes 786436
  49.8 6.4 %collective-permute-start = (f32[4,128,128]{2,1,0:T(8,128)S(1)}, f32[4,128,128]{2,1,0:T(8,128)S(1)}, u32[]{:S(2)}, u32[]{:S(2)}) collective-permute-start(f32[4,128,128]{2,1,0:T(8,128)S(1)} %get-tuple-element.41), channel_id=1, source_target_pairs={{0,4},{1,5},{2,6},{3,7},{4,0},{5,1},{6,2},{7,3},{8,12},{9,13},{10,... | collective-permute-start | bytes 786440 | tf_op jit(solution)/shard_map/ppermute | solution.py:363
  51.1 6.8 %collective-permute-start.5 = (f32[3,128,128]{2,1,0:T(8,128)S(1)}, f32[3,128,128]{2,1,0:T(8,128)S(1)}, u32[]{:S(2)}, u32[]{:S(2)}) collective-permute-start(f32[3,128,128]{2,1,0:T(8,128)S(1)} %add.90), channel_id=1, source_target_pairs={{0,8},{1,9},{2,10},{3,11},{4,12},{5,13},{6,14},{7,15},{8,0},{9,1},... | collective-permute-start | bytes 589832 | tf_op jit(solution)/shard_map/ppermute | solution.py:363
  52.7 49.2 %collective-permute-start.13 = (f32[2,128,1024]{2,1,0:T(8,128)S(1)}, f32[2,128,1024]{2,1,0:T(8,128)S(1)}, u32[]{:S(2)}, u32[]{:S(2)}) collective-permute-start(f32[2,128,1024]{2,1,0:T(8,128)S(1)} %value_grads.4.refs_0_), channel_id=1, source_target_pairs={{0,1},{1,0},{2,3},{3,2},{4,5},{5,4},{6,7},{7,6},{8,9},{9,8},{10,11... | collective-permute-start | bytes 3145736 | tf_op jit(solution)/shard_map/ppermute | solution.py:363
  56.3 10.8 %collective-permute-start.1 = (f32[4,128,128]{2,1,0:T(8,128)S(1)}, f32[4,128,128]{2,1,0:T(8,128)S(1)}, u32[]{:S(2)}, u32[]{:S(2)}) collective-permute-start(f32[4,128,128]{2,1,0:T(8,128)S(1)} %add.85), channel_id=1, source_target_pairs={{0,8},{1,9},{2,10},{3,11},{4,12},{5,13},{6,14},{7,15},{8,0},{9,1},... | collective-permute-start | bytes 786440 | tf_op jit(solution)/shard_map/ppermute | solution.py:363
  58.0 11.1 %collective-permute-start.6 = (f32[3,128,128]{2,1,0:T(8,128)S(1)}, f32[3,128,128]{2,1,0:T(8,128)S(1)}, u32[]{:S(2)}, u32[]{:S(2)}) collective-permute-start(f32[3,128,128]{2,1,0:T(8,128)S(1)} %add.91), channel_id=1, source_target_pairs={{0,16},{1,17},{2,18},{3,19},{4,20},{5,21},{6,22},{7,23},{8,24},{9,... | collective-permute-start | bytes 589832 | tf_op jit(solution)/shard_map/ppermute | solution.py:363
  63.2 44.1 %collective-permute-start.14 = (f32[2,128,1024]{2,1,0:T(8,128)S(1)}, f32[2,128,1024]{2,1,0:T(8,128)S(1)}, u32[]{:S(2)}, u32[]{:S(2)}) collective-permute-start(f32[2,128,1024]{2,1,0:T(8,128)S(1)} %collective-permute-done.12.refs_1_), channel_id=1, source_target_pairs={{0,1},{1,0},{2,3},{3,2},{4,5},{5,4},{6,7},{7,6},{8,9},{9,8},{10,11... | collective-permute-start | bytes 3145736 | tf_op jit(solution)/shard_map/ppermute | solution.py:363
  64.5 49.2 %collective-permute-start.29 = (f32[1024,256]{1,0:T(8,128)S(1)}, f32[1024,256]{1,0:T(8,128)S(1)}, u32[]{:S(2)}, u32[]{:S(2)}) collective-permute-start(f32[1024,256]{1,0:T(8,128)S(1)} %get-tuple-element.78), channel_id=1, source_target_pairs={{0,8},{1,9},{2,10},{3,11},{4,12},{5,13},{6,14},{7,15},{8,0},{9,1},... | collective-permute-start | bytes 3145736 | tf_op jit(solution)/shard_map/ppermute | solution.py:363
  67.2 30.7 %copy-start.35 = (f32[4,128,128]{2,1,0:T(8,128)}, f32[4,128,128]{2,1,0:T(8,128)S(1)}, u32[]{:S(2)}) copy-start(f32[4,128,128]{2,1,0:T(8,128)S(1)} %collective-permute-done.1) | copy-start | bytes 786436
  67.2 28.7 %collective-permute-start.2 = (f32[4,128,128]{2,1,0:T(8,128)S(1)}, f32[4,128,128]{2,1,0:T(8,128)S(1)}, u32[]{:S(2)}, u32[]{:S(2)}) collective-permute-start(f32[4,128,128]{2,1,0:T(8,128)S(1)} %add.86), channel_id=1, source_target_pairs={{0,16},{1,17},{2,18},{3,19},{4,20},{5,21},{6,22},{7,23},{8,24},{9,... | collective-permute-start | bytes 786440 | tf_op jit(solution)/shard_map/ppermute | solution.py:363
  69.2 28.4 %collective-permute-start.7 = (f32[3,128,128]{2,1,0:T(8,128)S(1)}, f32[3,128,128]{2,1,0:T(8,128)S(1)}, u32[]{:S(2)}, u32[]{:S(2)}) collective-permute-start(f32[3,128,128]{2,1,0:T(8,128)S(1)} %get-tuple-element.97), channel_id=1, source_target_pairs={{0,4},{1,5},{2,6},{3,7},{4,0},{5,1},{6,2},{7,3},{8,12},{9,13},{10,... | collective-permute-start | bytes 589832 | tf_op jit(solution)/shard_map/ppermute | solution.py:363
  95.9 26.2 %collective-permute-start.30 = (f32[1024,256]{1,0:T(8,128)S(1)}, f32[1024,256]{1,0:T(8,128)S(1)}, u32[]{:S(2)}, u32[]{:S(2)}) collective-permute-start(f32[1024,256]{1,0:T(8,128)S(1)} %get-tuple-element.75), channel_id=1, source_target_pairs={{0,8},{1,9},{2,10},{3,11},{4,12},{5,13},{6,14},{7,15},{8,0},{9,1},... | collective-permute-start | bytes 3145736 | tf_op jit(solution)/shard_map/ppermute | solution.py:363
  97.6 46.0 %collective-permute-start.25 = (f32[1024,256]{1,0:T(8,128)S(1)}, f32[1024,256]{1,0:T(8,128)S(1)}, u32[]{:S(2)}, u32[]{:S(2)}) collective-permute-start(f32[1024,256]{1,0:T(8,128)S(1)} %get-tuple-element.77), channel_id=1, source_target_pairs={{0,8},{1,9},{2,10},{3,11},{4,12},{5,13},{6,14},{7,15},{8,0},{9,1},... | collective-permute-start | bytes 3145736 | tf_op jit(solution)/shard_map/ppermute | solution.py:363
  101.9 48.2 %collective-permute-start.41 = (f32[2,128,1024]{2,1,0:T(8,128)S(1)}, f32[2,128,1024]{2,1,0:T(8,128)S(1)}, u32[]{:S(2)}, u32[]{:S(2)}) collective-permute-start(f32[2,128,1024]{2,1,0:T(8,128)S(1)} %value_grads.7), channel_id=1, source_target_pairs={{1,8},{3,10},{5,12},{7,14},{8,1},{10,3},{12,5},{14,7},{17,24},{19,... | collective-permute-start | bytes 3145736 | tf_op jit(solution)/shard_map/ppermute | solution.py:363
  103.3 12.5 %copy-start.29 = (bf16[1024,1024]{1,0:T(8,128)(2,1)}, bf16[1024,1024]{1,0:T(8,128)(2,1)S(1)}, u32[]{:S(2)}) copy-start(bf16[1024,1024]{1,0:T(8,128)(2,1)S(1)} %get-tuple-element.50.refs_4_) | copy-start | bytes 6291460
  103.3 12.5 %copy-start.31 = (bf16[1024,1024]{1,0:T(8,128)(2,1)}, bf16[1024,1024]{1,0:T(8,128)(2,1)S(1)}, u32[]{:S(2)}) copy-start(bf16[1024,1024]{1,0:T(8,128)(2,1)S(1)} %get-tuple-element.51.refs_5_) | copy-start | bytes 6291460
  107.3 45.5 %collective-permute-start.33 = (f32[2,128,1024]{2,1,0:T(8,128)S(1)}, f32[2,128,1024]{2,1,0:T(8,128)S(1)}, u32[]{:S(2)}, u32[]{:S(2)}) collective-permute-start(f32[2,128,1024]{2,1,0:T(8,128)S(1)} %value_grads.6), channel_id=1, source_target_pairs={{1,8},{3,10},{5,12},{7,14},{8,1},{10,3},{12,5},{14,7},{17,24},{19,... | collective-permute-start | bytes 3145736 | tf_op jit(solution)/shard_map/ppermute | solution.py:363
  113.8 40.6 %collective-permute-start.18 = (f32[2,2,128,512]{3,2,1,0:T(8,128)S(1)}, f32[2,2,128,512]{3,2,1,0:T(8,128)S(1)}, u32[]{:S(2)}, u32[]{:S(2)}) collective-permute-start(f32[2,2,128,512]{3,2,1,0:T(8,128)S(1)} %get-tuple-element.55), channel_id=1, source_target_pairs={{0,4},{1,5},{2,6},{3,7},{4,0},{5,1},{6,2},{7,3},{8,12},{9,13},{10,... | collective-permute-start | bytes 3145736 | tf_op jit(solution)/shard_map/ppermute | solution.py:363
  123.0 36.0 %collective-permute-start.15 = (f32[2,2,128,512]{3,2,1,0:T(8,128)}, f32[2,2,128,512]{3,2,1,0:T(8,128)}, u32[]{:S(2)}, u32[]{:S(2)}) collective-permute-start(f32[2,2,128,512]{3,2,1,0:T(8,128)} %get-tuple-element.53), channel_id=1, source_target_pairs={{0,4},{1,5},{2,6},{3,7},{4,0},{5,1},{6,2},{7,3},{8,12},{9,13},{10,... | collective-permute-start | bytes 3145736 | tf_op jit(solution)/shard_map/ppermute | solution.py:363
  143.6 47.5 %collective-permute-start.26 = (f32[1024,256]{1,0:T(8,128)}, f32[1024,256]{1,0:T(8,128)}, u32[]{:S(2)}, u32[]{:S(2)}) collective-permute-start(f32[1024,256]{1,0:T(8,128)} %get-tuple-element.76), channel_id=1, source_target_pairs={{0,8},{1,9},{2,10},{3,11},{4,12},{5,13},{6,14},{7,15},{8,0},{9,1},... | collective-permute-start | bytes 3145736 | tf_op jit(solution)/shard_map/ppermute | solution.py:363
  150.1 43.0 %collective-permute-start.21 = (f32[2,128,1024]{2,1,0:T(8,128)S(1)}, f32[2,128,1024]{2,1,0:T(8,128)}, u32[]{:S(2)}, u32[]{:S(2)}) collective-permute-start(f32[2,128,1024]{2,1,0:T(8,128)S(1)} %value_grads.5), channel_id=1, source_target_pairs={{1,8},{3,10},{5,12},{7,14},{8,1},{10,3},{12,5},{14,7},{17,24},{19,... | collective-permute-start | bytes 3145736 | tf_op jit(solution)/shard_map/ppermute | solution.py:363
  152.8 53.7 %collective-permute-start.42 = (f32[2,128,1024]{2,1,0:T(8,128)}, f32[2,128,1024]{2,1,0:T(8,128)}, u32[]{:S(2)}, u32[]{:S(2)}) collective-permute-start(f32[2,128,1024]{2,1,0:T(8,128)} %broadcast_select_fusion.refs_0_), channel_id=1, source_target_pairs={{0,2},{1,3},{2,0},{3,1},{4,6},{5,7},{6,4},{7,5},{8,10},{9,11},{10,... | collective-permute-start | bytes 3145736 | tf_op jit(solution)/shard_map/ppermute | solution.py:363
  155.4 69.8 %collective-permute-start.34 = (f32[2,128,1024]{2,1,0:T(8,128)}, f32[2,128,1024]{2,1,0:T(8,128)}, u32[]{:S(2)}, u32[]{:S(2)}) collective-permute-start(f32[2,128,1024]{2,1,0:T(8,128)} %broadcast_select_fusion.1.refs_0_), channel_id=1, source_target_pairs={{0,2},{1,3},{2,0},{3,1},{4,6},{5,7},{6,4},{7,5},{8,10},{9,11},{10,... | collective-permute-start | bytes 3145736 | tf_op jit(solution)/shard_map/ppermute | solution.py:363
  156.9 27.0 %copy-start.16 = (f32[4,128,128]{2,1,0:T(8,128)S(1)}, f32[4,128,128]{2,1,0:T(8,128)}, u32[]{:S(2)}) copy-start(f32[4,128,128]{2,1,0:T(8,128)} %copy-done.15) | copy-start | bytes 786436
  156.9 56.6 %copy-start.10 = (f32[1024,1024]{1,0:T(8,128)S(1)}, f32[1024,1024]{1,0:T(8,128)}, u32[]{:S(2)}) copy-start(f32[1024,1024]{1,0:T(8,128)} %k.11) | copy-start | bytes 12582916
  158.6 54.9 %copy-start.3 = (f32[1024,1024]{1,0:T(8,128)S(1)}, f32[1024,1024]{1,0:T(8,128)}, u32[]{:S(2)}) copy-start(f32[1024,1024]{1,0:T(8,128)} %q.11) | copy-start | bytes 12582916
  158.6 54.9 %copy-start.7 = (f32[1024,1024]{1,0:T(8,128)S(1)}, f32[1024,1024]{1,0:T(8,128)}, u32[]{:S(2)}) copy-start(f32[1024,1024]{1,0:T(8,128)} %g.11) | copy-start | bytes 12582916
  158.6 54.9 %copy-start.24 = (f32[1,128,128]{2,1,0:T(8,128)S(1)}, f32[1,128,128]{2,1,0:T(8,128)}, u32[]{:S(2)}) copy-start(f32[1,128,128]{2,1,0:T(8,128)} %copy-done.23) | copy-start | bytes 196612
  158.6 54.9 %copy-start.26 = (f32[1,128,128]{2,1,0:T(8,128)S(1)}, f32[1,128,128]{2,1,0:T(8,128)}, u32[]{:S(2)}) copy-start(f32[1,128,128]{2,1,0:T(8,128)} %copy-done.25) | copy-start | bytes 196612
  159.1 54.5 %collective-permute-start.19 = (f32[1,2,128,512]{3,2,1,0:T(8,128)S(1)}, f32[1,2,128,512]{3,2,1,0:T(8,128)S(1)}, u32[]{:S(2)}, u32[]{:S(2)}) collective-permute-start(f32[1,2,128,512]{3,2,1,0:T(8,128)S(1)} %slice.117), channel_id=1, source_target_pairs={{0,8},{1,9},{2,10},{3,11},{4,12},{5,13},{6,14},{7,15},{8,0},{9,1},... | collective-permute-start | bytes 1572872 | tf_op jit(solution)/shard_map/ppermute | solution.py:363
  191.1 15.3 %collective-permute-start.3 = (f32[4,128,128]{2,1,0:T(8,128)S(1)}, f32[4,128,128]{2,1,0:T(8,128)S(1)}, u32[]{:S(2)}, u32[]{:S(2)}) collective-permute-start(f32[4,128,128]{2,1,0:T(8,128)S(1)} %get-tuple-element.95), channel_id=1, source_target_pairs={{0,4},{1,5},{2,6},{3,7},{4,0},{5,1},{6,2},{7,3},{8,12},{9,13},{10,... | collective-permute-start | bytes 786440 | tf_op jit(solution)/shard_map/ppermute | solution.py:363
  193.1 32.7 %collective-permute-start.16 = (f32[1,2,128,512]{3,2,1,0:T(8,128)S(1)}, f32[1,2,128,512]{3,2,1,0:T(8,128)S(1)}, u32[]{:S(2)}, u32[]{:S(2)}) collective-permute-start(f32[1,2,128,512]{3,2,1,0:T(8,128)S(1)} %slice.113), channel_id=1, source_target_pairs={{0,8},{1,9},{2,10},{3,11},{4,12},{5,13},{6,14},{7,15},{8,0},{9,1},... | collective-permute-start | bytes 1572872 | tf_op jit(solution)/shard_map/ppermute | solution.py:363
  206.5 19.5 %collective-permute-start.43 = (f32[2,128,1024]{2,1,0:T(8,128)}, f32[2,128,1024]{2,1,0:T(8,128)S(1)}, u32[]{:S(2)}, u32[]{:S(2)}) collective-permute-start(f32[2,128,1024]{2,1,0:T(8,128)} %broadcast_select_fusion.refs_0_), channel_id=1, source_target_pairs={{0,1},{1,0},{2,3},{3,2},{4,5},{5,4},{6,7},{7,6},{8,9},{9,8},{10,11... | collective-permute-start | bytes 3145736 | tf_op jit(solution)/shard_map/ppermute | solution.py:363
  206.5 25.6 %collective-permute-start.22 = (f32[2,128,1024]{2,1,0:T(8,128)S(1)}, f32[2,128,1024]{2,1,0:T(8,128)S(1)}, u32[]{:S(2)}, u32[]{:S(2)}) collective-permute-start(f32[2,128,1024]{2,1,0:T(8,128)S(1)} %broadcast_select_fusion.2.refs_0_), channel_id=1, source_target_pairs={{0,2},{1,3},{2,0},{3,1},{4,6},{5,7},{6,4},{7,5},{8,10},{9,11},{10,... | collective-permute-start | bytes 3145736 | tf_op jit(solution)/shard_map/ppermute | solution.py:363
  213.5 18.6 %collective-permute-start.44 = (f32[2,128,1024]{2,1,0:T(8,128)}, f32[2,128,1024]{2,1,0:T(8,128)S(1)}, u32[]{:S(2)}, u32[]{:S(2)}) collective-permute-start(f32[2,128,1024]{2,1,0:T(8,128)} %collective-permute-done.42.refs_1_), channel_id=1, source_target_pairs={{0,1},{1,0},{2,3},{3,2},{4,5},{5,4},{6,7},{7,6},{8,9},{9,8},{10,11... | collective-permute-start | bytes 3145736 | tf_op jit(solution)/shard_map/ppermute | solution.py:363
  222.5 12.3 %copy-start.30 = (bf16[1024,1024]{1,0:T(8,128)(2,1)S(1)}, bf16[1024,1024]{1,0:T(8,128)(2,1)}, u32[]{:S(2)}) copy-start(bf16[1024,1024]{1,0:T(8,128)(2,1)} %copy-done.29) | copy-start | bytes 6291460
  225.2 23.7 %collective-permute-start.35 = (f32[2,128,1024]{2,1,0:T(8,128)}, f32[2,128,1024]{2,1,0:T(8,128)S(1)}, u32[]{:S(2)}, u32[]{:S(2)}) collective-permute-start(f32[2,128,1024]{2,1,0:T(8,128)} %broadcast_select_fusion.1.refs_0_), channel_id=1, source_target_pairs={{0,1},{1,0},{2,3},{3,2},{4,5},{5,4},{6,7},{7,6},{8,9},{9,8},{10,11... | collective-permute-start | bytes 3145736 | tf_op jit(solution)/shard_map/ppermute | solution.py:363
  225.7 25.1 %collective-permute-start.36 = (f32[2,128,1024]{2,1,0:T(8,128)}, f32[2,128,1024]{2,1,0:T(8,128)S(1)}, u32[]{:S(2)}, u32[]{:S(2)}) collective-permute-start(f32[2,128,1024]{2,1,0:T(8,128)} %collective-permute-done.34.refs_1_), channel_id=1, source_target_pairs={{0,1},{1,0},{2,3},{3,2},{4,5},{5,4},{6,7},{7,6},{8,9},{9,8},{10,11... | collective-permute-start | bytes 3145736 | tf_op jit(solution)/shard_map/ppermute | solution.py:363
  226.0 39.0 %collective-permute-start.23 = (f32[2,128,1024]{2,1,0:T(8,128)S(1)}, f32[2,128,1024]{2,1,0:T(8,128)S(1)}, u32[]{:S(2)}, u32[]{:S(2)}) collective-permute-start(f32[2,128,1024]{2,1,0:T(8,128)S(1)} %broadcast_select_fusion.2.refs_0_), channel_id=1, source_target_pairs={{0,1},{1,0},{2,3},{3,2},{4,5},{5,4},{6,7},{7,6},{8,9},{9,8},{10,11... | collective-permute-start | bytes 3145736 | tf_op jit(solution)/shard_map/ppermute | solution.py:363
  232.1 34.9 %collective-permute-start.24 = (f32[2,128,1024]{2,1,0:T(8,128)S(1)}, f32[2,128,1024]{2,1,0:T(8,128)S(1)}, u32[]{:S(2)}, u32[]{:S(2)}) collective-permute-start(f32[2,128,1024]{2,1,0:T(8,128)S(1)} %collective-permute-done.22.refs_1_), channel_id=1, source_target_pairs={{0,1},{1,0},{2,3},{3,2},{4,5},{5,4},{6,7},{7,6},{8,9},{9,8},{10,11... | collective-permute-start | bytes 3145736 | tf_op jit(solution)/shard_map/ppermute | solution.py:363
  232.1 87.7 %collective-permute-start.20 = (f32[1,128,512]{2,1,0:T(8,128)S(1)}, f32[1,128,512]{2,1,0:T(8,128)S(1)}, u32[]{:S(2)}, u32[]{:S(2)}) collective-permute-start(f32[1,128,512]{2,1,0:T(8,128)S(1)} %get-tuple-element.91), channel_id=1, source_target_pairs={{0,16},{1,17},{2,18},{3,19},{4,20},{5,21},{6,22},{7,23},{8,24},{9,... | collective-permute-start | bytes 786440 | tf_op jit(solution)/shard_map/ppermute | solution.py:363
  248.9 30.4 %collective-permute-start.47 = (f32[2,128,512]{2,1,0:T(8,128)S(1)}, f32[2,128,512]{2,1,0:T(8,128)S(1)}, u32[]{:S(2)}, u32[]{:S(2)}) collective-permute-start(f32[2,128,512]{2,1,0:T(8,128)S(1)} %get-tuple-element.71), channel_id=1, source_target_pairs={{0,4},{1,5},{2,6},{3,7},{4,0},{5,1},{6,2},{7,3},{8,12},{9,13},{10,... | collective-permute-start | bytes 1572872 | tf_op jit(solution)/shard_map/ppermute | solution.py:363
  250.9 30.6 %collective-permute-start.45 = (f32[2,128,512]{2,1,0:T(8,128)S(1)}, f32[2,128,512]{2,1,0:T(8,128)S(1)}, u32[]{:S(2)}, u32[]{:S(2)}) collective-permute-start(f32[2,128,512]{2,1,0:T(8,128)S(1)} %get-tuple-element.69), channel_id=1, source_target_pairs={{0,4},{1,5},{2,6},{3,7},{4,0},{5,1},{6,2},{7,3},{8,12},{9,13},{10,... | collective-permute-start | bytes 1572872 | tf_op jit(solution)/shard_map/ppermute | solution.py:363
  265.0 21.2 %collective-permute-start.39 = (f32[2,128,512]{2,1,0:T(8,128)S(1)}, f32[2,128,512]{2,1,0:T(8,128)S(1)}, u32[]{:S(2)}, u32[]{:S(2)}) collective-permute-start(f32[2,128,512]{2,1,0:T(8,128)S(1)} %get-tuple-element.67), channel_id=1, source_target_pairs={{0,4},{1,5},{2,6},{3,7},{4,0},{5,1},{6,2},{7,3},{8,12},{9,13},{10,... | collective-permute-start | bytes 1572872 | tf_op jit(solution)/shard_map/ppermute | solution.py:363
  267.0 30.4 %collective-permute-start.37 = (f32[2,128,512]{2,1,0:T(8,128)S(1)}, f32[2,128,512]{2,1,0:T(8,128)S(1)}, u32[]{:S(2)}, u32[]{:S(2)}) collective-permute-start(f32[2,128,512]{2,1,0:T(8,128)S(1)} %get-tuple-element.65), channel_id=1, source_target_pairs={{0,4},{1,5},{2,6},{3,7},{4,0},{5,1},{6,2},{7,3},{8,12},{9,13},{10,... | collective-permute-start | bytes 1572872 | tf_op jit(solution)/shard_map/ppermute | solution.py:363
  279.3 29.4 %collective-permute-start.31 = (f32[2,128,512]{2,1,0:T(8,128)S(1)}, f32[2,128,512]{2,1,0:T(8,128)S(1)}, u32[]{:S(2)}, u32[]{:S(2)}) collective-permute-start(f32[2,128,512]{2,1,0:T(8,128)S(1)} %get-tuple-element.63), channel_id=1, source_target_pairs={{0,4},{1,5},{2,6},{3,7},{4,0},{5,1},{6,2},{7,3},{8,12},{9,13},{10,... | collective-permute-start | bytes 1572872 | tf_op jit(solution)/shard_map/ppermute | solution.py:363
  281.4 41.0 %collective-permute-start.17 = (f32[1,128,512]{2,1,0:T(8,128)S(1)}, f32[1,128,512]{2,1,0:T(8,128)S(1)}, u32[]{:S(2)}, u32[]{:S(2)}) collective-permute-start(f32[1,128,512]{2,1,0:T(8,128)S(1)} %get-tuple-element.93), channel_id=1, source_target_pairs={{0,16},{1,17},{2,18},{3,19},{4,20},{5,21},{6,22},{7,23},{8,24},{9,... | collective-permute-start | bytes 786440 | tf_op jit(solution)/shard_map/ppermute | solution.py:363
  286.2 33.1 %collective-permute-start.27 = (f32[2,128,512]{2,1,0:T(8,128)S(1)}, f32[2,128,512]{2,1,0:T(8,128)S(1)}, u32[]{:S(2)}, u32[]{:S(2)}) collective-permute-start(f32[2,128,512]{2,1,0:T(8,128)S(1)} %get-tuple-element.59), channel_id=1, source_target_pairs={{0,4},{1,5},{2,6},{3,7},{4,0},{5,1},{6,2},{7,3},{8,12},{9,13},{10,... | collective-permute-start | bytes 1572872 | tf_op jit(solution)/shard_map/ppermute | solution.py:363
  288.3 37.1 %copy-start.13 = (f32[1024,1024]{1,0:T(8,128)S(1)}, f32[1024,1024]{1,0:T(8,128)}, u32[]{:S(2)}) copy-start(f32[1024,1024]{1,0:T(8,128)} %v.3) | copy-start | bytes 12582916
  297.4 25.3 %collective-permute-start.48 = (f32[1,128,512]{2,1,0:T(8,128)S(1)}, f32[1,128,512]{2,1,0:T(8,128)S(1)}, u32[]{:S(2)}, u32[]{:S(2)}) collective-permute-start(f32[1,128,512]{2,1,0:T(8,128)S(1)} %get-tuple-element.79), channel_id=1, source_target_pairs={{0,16},{1,17},{2,18},{3,19},{4,20},{5,21},{6,22},{7,23},{8,24},{9,... | collective-permute-start | bytes 786440 | tf_op jit(solution)/shard_map/ppermute | solution.py:363
  308.7 32.3 %collective-permute-start.46 = (f32[1,128,512]{2,1,0:T(8,128)S(1)}, f32[1,128,512]{2,1,0:T(8,128)S(1)}, u32[]{:S(2)}, u32[]{:S(2)}) collective-permute-start(f32[1,128,512]{2,1,0:T(8,128)S(1)} %get-tuple-element.81), channel_id=1, source_target_pairs={{0,16},{1,17},{2,18},{3,19},{4,20},{5,21},{6,22},{7,23},{8,24},{9,... | collective-permute-start | bytes 786440 | tf_op jit(solution)/shard_map/ppermute | solution.py:363
  319.3 31.6 %collective-permute-start.40 = (f32[1,128,512]{2,1,0:T(8,128)S(1)}, f32[1,128,512]{2,1,0:T(8,128)S(1)}, u32[]{:S(2)}, u32[]{:S(2)}) collective-permute-start(f32[1,128,512]{2,1,0:T(8,128)S(1)} %get-tuple-element.83), channel_id=1, source_target_pairs={{0,16},{1,17},{2,18},{3,19},{4,20},{5,21},{6,22},{7,23},{8,24},{9,... | collective-permute-start | bytes 786440 | tf_op jit(solution)/shard_map/ppermute | solution.py:363
  319.8 36.7 %collective-permute-start.38 = (f32[1,128,512]{2,1,0:T(8,128)S(1)}, f32[1,128,512]{2,1,0:T(8,128)S(1)}, u32[]{:S(2)}, u32[]{:S(2)}) collective-permute-start(f32[1,128,512]{2,1,0:T(8,128)S(1)} %get-tuple-element.85), channel_id=1, source_target_pairs={{0,16},{1,17},{2,18},{3,19},{4,20},{5,21},{6,22},{7,23},{8,24},{9,... | collective-permute-start | bytes 786440 | tf_op jit(solution)/shard_map/ppermute | solution.py:363
  322.5 39.7 %collective-permute-start.32 = (f32[1,128,512]{2,1,0:T(8,128)S(1)}, f32[1,128,512]{2,1,0:T(8,128)S(1)}, u32[]{:S(2)}, u32[]{:S(2)}) collective-permute-start(f32[1,128,512]{2,1,0:T(8,128)S(1)} %get-tuple-element.87), channel_id=1, source_target_pairs={{0,16},{1,17},{2,18},{3,19},{4,20},{5,21},{6,22},{7,23},{8,24},{9,... | collective-permute-start | bytes 786440 | tf_op jit(solution)/shard_map/ppermute | solution.py:363
  322.8 44.5 %collective-permute-start.28 = (f32[1,128,512]{2,1,0:T(8,128)S(1)}, f32[1,128,512]{2,1,0:T(8,128)S(1)}, u32[]{:S(2)}, u32[]{:S(2)}) collective-permute-start(f32[1,128,512]{2,1,0:T(8,128)S(1)} %get-tuple-element.89), channel_id=1, source_target_pairs={{0,16},{1,17},{2,18},{3,19},{4,20},{5,21},{6,22},{7,23},{8,24},{9,... | collective-permute-start | bytes 786440 | tf_op jit(solution)/shard_map/ppermute | solution.py:363
  325.4 41.9 %copy-start.27 = (f32[1,1024]{1,0:T(1,128)S(1)}, f32[1,1024]{1,0:T(1,128)}, u32[]{:S(2)}) copy-start(f32[1,1024]{1,0:T(1,128)} %col_state.1) | copy-start | bytes 12292
  325.4 41.9 %copy-start.28 = (f32[1,512]{1,0:T(1,128)S(1)}, f32[1,512]{1,0:T(1,128)}, u32[]{:S(2)}) copy-start(f32[1,512]{1,0:T(1,128)} %row_state.1) | copy-start | bytes 6148
  (22 other events, 100.2 us)
where the time goes:
time: 371 us; the launch traced here: 370 us
  waiting for transfers between devices  137 us (37%)
  Pallas kernels  107 us (29%)
  starting transfers between devices  101 us (27%)
  local copies, waits for them, and re-layouts  18.2 us (5%)
  other arithmetic  6.52 us (2%)
    ppermute x49, waiting for transfers between devices, permute(): return lax.ppermute(x, AXES, pairs)  137 us
    ppermute x49, starting transfers between devices, permute(): return lax.ppermute(x, AXES, pairs)  101 us
    pallas_call x8, Pallas kernels, weight_parts(): pl.pallas_call(functools.partial(weight_body, ny, low, counts), grid_spec...  52 us
    pallas_call x2, Pallas kernels, query_key_grads(): pl.pallas_call(functools.partial(query_key_body, scale, blk), grid_spec=p...  21.9 us
    unnamed x74, local copies, waits for them, and re-layouts  16.4 us
    pallas_call x4, Pallas kernels, value_grads(): pl.pallas_call(functools.partial(value_body, scale, blk), grid_spec=pltpu...  15.9 us
    pallas_call x3, Pallas kernels, outer_sums(): pl.pallas_call(functools.partial(outer_body, low), grid_spec=pltpu.Prefet...  10 us
  transfers between devices with their start and end apart: 49, of which 21 were waited for; matrix products, arithmetic and copies ran while one was open for 2% of the time, Pallas kernels for 26%

commit v1 on v0

--- a/solution.py
+++ b/solution.py
@@ -1,4 +1,5 @@
 import functools
+import math
 import jax
 import jax.numpy as jnp
 from jax import lax
@@ -14,7 +15,7 @@
 BF16 = jnp.bfloat16
 AXES = ("seq", "head")
 ALONE = 1
-PIECES = ((2, 2), (2, 2))
+PIECES = ((1, 1, 1, 1), (2, 2))
 SPLIT = (0, 1, 2, 3)
 NN = (((1,), (0,)), ((), ()))
 NT = (((1,), (1,)), ((), ()))
@@ -178,25 +179,27 @@
     )(scal, q, k, v, g, *fwd, *rev, *filled)
 
 
-def terms_body(*refs):
+def terms_body(blk, *refs):
     pieces, (hi, lo) = refs[:-2], refs[-2:]
     at = 0
     for ref in pieces:
-        cols = pl.ds(at, ref.shape[1])
-        hi[:, cols], lo[:, cols] = split(ref[...])
-        at += ref.shape[1]
-
-
-def split_terms(pieces):
+        for begin in range(0, ref.shape[1], min(blk, ref.shape[1])):
+            size = min(blk, ref.shape[1] - begin)
+            where = (at // blk, slice(None), pl.ds(at % blk, size))
+            hi[where], lo[where] = split(ref[:, pl.ds(begin, size)])
+            at += size
+
+
+def split_terms(pieces, blk):
     tokens, width = pieces[0].shape[0], sum(x.shape[1] for x in pieces)
-    blk = min(256, tokens)
-    spec = pl.BlockSpec((blk, width), lambda n: (n, 0))
-    return pl.pallas_call(
-        terms_body,
-        grid=(tokens // blk,),
-        in_specs=[pl.BlockSpec((blk, x.shape[1]), lambda n: (n, 0)) for x in pieces],
+    rows = min(256, tokens)
+    spec = pl.BlockSpec((width // blk, rows, blk), lambda n: (0, n, 0))
+    return pl.pallas_call(
+        functools.partial(terms_body, blk),
+        grid=(tokens // rows,),
+        in_specs=[pl.BlockSpec((rows, x.shape[1]), lambda n: (n, 0)) for x in pieces],
         out_specs=[spec] * 2,
-        out_shape=[jax.ShapeDtypeStruct((tokens, width), BF16)] * 2,
+        out_shape=[jax.ShapeDtypeStruct((width // blk, tokens, blk), BF16)] * 2,
         compiler_params=params(),
         cost_estimate=cost(4 * tokens * width, 8 * tokens * width),
         name="split_terms",
@@ -219,18 +222,18 @@
     first = scal[0] == 1
     a, b = [x[0] for x in mine], [x[0] for x in other]
     if far:
-        far_hi, far_lo, at = far[0][...], far[1][...], 0
+        far_hi, far_lo, at = far[0][0], far[1][0], 0
         for c in range(1, len(counts)):
             at += counts[c - 1]
             later = pl.program_id(1) >= at
-            far_hi = jnp.where(later, far[2 * c][...], far_hi)
-            far_lo = jnp.where(later, far[2 * c + 1][...], far_lo)
+            far_hi = jnp.where(later, far[2 * c][0], far_hi)
+            far_lo = jnp.where(later, far[2 * c + 1][0], far_lo)
         own_rows = [jnp.where(first, x, y) for x, y in zip(a, b)]
         far_rows = [jnp.where(first, y, x) for x, y in zip(a, b)]
-        total = rows_times(own_rows, own_hi[...], own_lo[...]) + rows_times(far_rows, far_hi, far_lo)
+        total = rows_times(own_rows, own_hi[0], own_lo[0]) + rows_times(far_rows, far_hi, far_lo)
         places = [(scal[2] ^ n,) for n in range(ny)]
     else:
-        total = rows_times(a + b, own_hi[...], own_lo[...])
+        total = rows_times(a + b, own_hi[0], own_lo[0])
         places = [(1 - scal[0], scal[2] ^ n) for n in range(ny)]
         places += [(scal[0], scal[2] ^ n) for n in range(ny)]
     height = total.shape[0] // len(places)
@@ -245,17 +248,16 @@
 def weight_parts(scal, mine, other, own, fars, offset, width):
     ny = len(mine)
     low, height, tokens = mine[0].shape
-    widths = [x[0].shape[1] for x in fars] or [width]
-    blk = 256 if all(x % 256 == 0 for x in widths + [offset]) else 128
-    counts = [x // blk for x in widths]
+    blk = own[0].shape[2]
+    counts = [x[0].shape[0] for x in fars]
     count, first = width // blk, offset // blk
     lead = (ny, height) if fars else (2, ny, height)
     grad_spec = pl.BlockSpec((1, height, tokens), lambda p, n, s: (s[1] ^ (low - 1 - p), 0, 0))
-    own_spec = pl.BlockSpec((tokens, blk), lambda p, n, s: (0, n + first))
+    own_spec = pl.BlockSpec((1, tokens, blk), lambda p, n, s: (n + first, 0, 0))
 
     def far_spec(c):
         begin = sum(counts[:c])
-        return pl.BlockSpec((tokens, blk), lambda p, n, s: (0, jnp.clip(n - begin, 0, counts[c] - 1)))
+        return pl.BlockSpec((1, tokens, blk), lambda p, n, s: (jnp.clip(n - begin, 0, counts[c] - 1), 0, 0))
 
     def out_spec(jj):
         col = by_phase(low - 1 - jj, count)
@@ -379,7 +381,8 @@
         got = over_seq(send, 1)
         total, enter, bit = keep + got, jnp.zeros_like(keep), low
         while bit < n_seq:
-            came = over_seq(total, bit)
+            wanted = lambda s: 2 * bit < n_seq or bool(s & bit) == reverse
+            came = permute(total, lambda s, h: (s ^ bit, h) if wanted(s) else None)
             take = ((seq & bit) == 0) if reverse else ((seq & bit) != 0)
             enter = enter + jnp.where(take, came, 0.0)
             bit *= 2
@@ -392,7 +395,9 @@
 
     sums = outer_sums(scal, queries, out_grad, low, chunks, 0, 1)
     rest = outer_sums(scal, queries, out_grad, low, chunks, 1, chunks - 1)
-    own_terms = split_terms([inputs])
+    parts = [sum(sizes) * inputs.shape[1] // 8 for sizes in PIECES]
+    blk = math.gcd(256, *parts)
+    own_terms = split_terms([inputs], blk)
     rev0 = scan_states(sums, True)
     rev1 = scan_states(rest, True)
     fwd = scan_states(outer_sums(scal, values, keys, low, chunks, 0, chunks), False)
@@ -404,7 +409,7 @@
             piece = inputs[:, at * eighth : (at + size) * eighth]
             pieces.append(over_seq(piece, low))
             at = at + size
-        far_terms.append(split_terms(pieces))
+        far_terms.append(split_terms(pieces, blk))
 
     def state_of(a):
         return (rev0, 0) if a == 0 else (rev1, a - 1)
@@ -437,7 +442,7 @@
         row, offset = [], 0
         groups = [[x] for x in far_terms] if a in SPLIT else [far_terms]
         for fars in groups:
-            size = sum(x[0].shape[1] for x in fars)
+            size = blk * sum(x[0].shape[0] for x in fars)
             keep, send = weight_parts(
                 scal, *gathered[a], own_terms,
                 fars if a >= ALONE else [], offset, size,

time: 371 us -> 375 us (1.011)
  waiting for transfers between devices: 137 us -> 167 us
  starting transfers between devices: 101 us -> 76.5 us
  Pallas kernels: 107 us -> 102 us
    ppermute x49 -> x51, waiting for transfers between devices: 137 us -> 167 us  [permute(): return lax.ppermute(x, AXES, pairs)]
    ppermute x49 -> x51, starting transfers between devices: 101 us -> 76.5 us  [permute(): return lax.ppermute(x, AXES, pairs)]
    pallas_call x8, Pallas kernels: 52 us -> 47 us  [weight_parts(): pl.pallas_call(functools.partial(weight_body, ny, low, counts), grid_spec...]
    unnamed x74 -> x88, local copies, waits for them, and re-layouts: 16.4 us -> 18.4 us
  transfers between devices with their start and end apart: 49 -> 51, of which waited for: 21 -> 23; matrix products, arithmetic and copies ran while one was open for 2% -> 2% of each run, Pallas kernels for 26% -> 25%
where the time goes in v1:
time: 375 us; the launch traced here: 374 us
  waiting for transfers between devices  167 us (45%)
  Pallas kernels  102 us (27%)
  starting transfers between devices  76.5 us (20%)
  local copies, waits for them, and re-layouts  20.1 us (5%)
  other arithmetic  6.6 us (2%)
    ppermute x51, waiting for transfers between devices, permute(): return lax.ppermute(x, AXES, pairs)  167 us
    ppermute x51, starting transfers between devices, permute(): return lax.ppermute(x, AXES, pairs)  76.5 us
    pallas_call x8, Pallas kernels, weight_parts(): pl.pallas_call(functools.partial(weight_body, ny, low, counts), grid_spec...  47 us
    pallas_call x2, Pallas kernels, query_key_grads(): pl.pallas_call(functools.partial(query_key_body, scale, blk), grid_spec=p...  21.7 us
    unnamed x88, local copies, waits for them, and re-layouts  18.4 us
    pallas_call x4, Pallas kernels, value_grads(): pl.pallas_call(functools.partial(value_body, scale, blk), grid_spec=pltpu...  15.9 us
    pallas_call x3, Pallas kernels, outer_sums(): pl.pallas_call(functools.partial(outer_body, low), grid_spec=pltpu.Prefet...  10 us
  transfers between devices with their start and end apart: 51, of which 23 were waited for; matrix products, arithmetic and copies ran while one was open for 2% of the time, Pallas kernels for 25%

profile of v1, /device:TPU:0, one launch (start us, length us, event | category | flops | bytes accessed | tf_op | source)
XLA Modules:
  0.0 373.6 jit_solution(403910688742660756)
XLA Ops:
  0.7 2.2 copy-done
  2.9 2.2 copy-done.4
  5.1 1.6 outer_sums.5
  6.7 3.0 collective-permute-start.8
  9.8 2.2 collective-permute-done.8
  12.0 2.2 collective-permute-start.9
  14.2 2.2 collective-permute-done.9
  17.8 5.7 %collective-permute-done.10 = f32[1,128,128]{2,1,0:T(8,128)S(1)} collective-permute-done((f32[1,128,128]{2,1,0:T(8,128)S(1)}, f32[1,128,128]{2,1,0:T(8,128)S(1)}, u32[]{:S(2)}, u32[]{:S(2)}) %collective-permute-start.10) | collective-permute-done | bytes 65568 | tf_op jit(solution)/shard_map/ppermute | solution.py:365
  23.6 2.0 collective-permute-start.11
  25.6 2.3 collective-permute-done.11.rev_other.other
  27.9 2.2 copy-done.1
  30.1 2.2 copy-done.5
  32.3 2.2 copy-done.8
  34.5 4.0 %value_grads.4.refs_0_ = f32[2,128,1024]{2,1,0:T(8,128)S(1)} custom-call(s32[3]{0:T(128)S(1)} %pad_add_fusion.scal, f32[1024,1024]{1,0:T(8,128)S(1)} %copy-done.1, f32[1024,1024]{1,0:T(8,128)S(1)} %copy-done.8, f32[1024,1024]{1,0:T(8,128)S(1)} %copy-done.5, f32[1,128,128]{2,1,0:T(8,128)S(1)} %get-tuple-element.102.rev.mine, ...), custom_call_target="tpu_custom_call" | custom-call | flops 805306368 | bytes 4194304 | tf_op jit(solution)/shard_map/value_grads/pallas_call | solution.py:122
  38.5 2.0 collective-permute-start.12
  40.5 3.7 outer_sums.4
  45.8 4.2 %collective-permute-done.4 = f32[3,128,128]{2,1,0:T(8,128)S(1)} collective-permute-done((f32[3,128,128]{2,1,0:T(8,128)S(1)}, f32[3,128,128]{2,1,0:T(8,128)S(1)}, u32[]{:S(2)}, u32[]{:S(2)}) %collective-permute-start.4) | collective-permute-done | bytes 196640 | tf_op jit(solution)/shard_map/ppermute | solution.py:365
  50.0 1.6 collective-permute-start.5
  52.3 4.7 %outer_sums.3 = (f32[4,128,128]{2,1,0:T(8,128)S(1)}, f32[4,128,128]{2,1,0:T(8,128)S(1)}) custom-call(s32[3]{0:T(128)S(1)} %pad_add_fusion.scal, f32[1024,1024]{1,0:T(8,128)S(1)} %copy-done.11, f32[1024,1024]{1,0:T(8,128)S(1)} %copy-done.9), custom_call_target="tpu_custom_call" | custom-call | flops 805306368 | bytes 8388608 | tf_op jit(solution)/shard_map/outer_sums/pallas_call | solution.py:87
  60.7 4.9 %collective-permute-done = f32[4,128,128]{2,1,0:T(8,128)S(1)} collective-permute-done((f32[4,128,128]{2,1,0:T(8,128)S(1)}, f32[4,128,128]{2,1,0:T(8,128)S(1)}, u32[]{:S(2)}, u32[]{:S(2)}) %collective-permute-start) | collective-permute-done | bytes 262176 | tf_op jit(solution)/shard_map/ppermute | solution.py:365
  65.6 1.6 collective-permute-start.26
  67.2 6.7 %collective-permute-done.6 = f32[3,128,128]{2,1,0:T(8,128)S(1)} collective-permute-done((f32[3,128,128]{2,1,0:T(8,128)S(1)}, f32[3,128,128]{2,1,0:T(8,128)S(1)}, u32[]{:S(2)}, u32[]{:S(2)}) %collective-permute-start.6) | collective-permute-done | bytes 196640 | tf_op jit(solution)/shard_map/ppermute | solution.py:365
  74.0 1.8 collective-permute-start.7
  76.9 6.4 %collective-permute-done.26.refs_1_ = f32[1024,128]{1,0:T(8,128)S(1)} collective-permute-done((f32[1024,128]{1,0:T(8,128)S(1)}, f32[1024,128]{1,0:T(8,128)S(1)}, u32[]{:S(2)}, u32[]{:S(2)}) %collective-permute-start.26) | collective-permute-done | bytes 524320 | tf_op jit(solution)/shard_map/ppermute | solution.py:365
  83.3 5.6 %collective-permute-done.1 = f32[4,128,128]{2,1,0:T(8,128)S(1)} collective-permute-done((f32[4,128,128]{2,1,0:T(8,128)S(1)}, f32[4,128,128]{2,1,0:T(8,128)S(1)}, u32[]{:S(2)}, u32[]{:S(2)}) %collective-permute-start.1) | collective-permute-done | bytes 262176 | tf_op jit(solution)/shard_map/ppermute | solution.py:365
  88.9 2.0 collective-permute-start.28
  91.0 4.0 %value_grads.7 = f32[2,128,1024]{2,1,0:T(8,128)S(1)} custom-call(s32[3]{0:T(128)S(1)} %pad_add_fusion.scal, f32[1024,1024]{1,0:T(8,128)S(1)} %copy-done.2, f32[1024,1024]{1,0:T(8,128)S(1)} %copy-done.9, f32[1024,1024]{1,0:T(8,128)S(1)} %copy-done.6, f32[3,128,128]{2,1,0:T(8,128)S(1)} %get-tuple-element.100.rev.mine, ...), custom_call_target="tpu_custom_call" | custom-call | flops 805306368 | bytes 4194304 | tf_op jit(solution)/shard_map/value_grads/pallas_call | solution.py:122
  96.8 4.0 %value_grads.6 = f32[2,128,1024]{2,1,0:T(8,128)S(1)} custom-call(s32[3]{0:T(128)S(1)} %pad_add_fusion.scal, f32[1024,1024]{1,0:T(8,128)S(1)} %copy-done.2, f32[1024,1024]{1,0:T(8,128)S(1)} %copy-done.9, f32[1024,1024]{1,0:T(8,128)S(1)} %copy-done.6, f32[3,128,128]{2,1,0:T(8,128)S(1)} %get-tuple-element.100.rev.mine, ...), custom_call_target="tpu_custom_call" | custom-call | flops 805306368 | bytes 4194304 | tf_op jit(solution)/shard_map/value_grads/pallas_call | solution.py:122
  101.5 4.9 %weight_parts.9 = (f32[2,2,128,512]{3,2,1,0:T(8,128)S(1)}, f32[2,2,128,512]{3,2,1,0:T(8,128)S(1)}) custom-call(s32[3]{0:T(128)S(1)} %pad_add_fusion.scal, f32[2,128,1024]{2,1,0:T(8,128)S(1)} %value_grads.4.refs_0_, f32[2,128,1024]{2,1,0:T(8,128)S(1)} %collective-permute-done.12.refs_1_, f32[2,128,1024]{2,1,0:T(8,128)S(1)} %collective-permute-done.13.refs_2_, ...), custom_call_target="tpu_custom_call" | custom-call | flops 3221225472 | bytes 9437184 | tf_op jit(solution)/shard_map/weight_parts/pallas_call | solution.py:267
  106.5 16.2 %collective-permute-done.27.refs_2_ = f32[1024,128]{1,0:T(8,128)S(1)} collective-permute-done((f32[1024,128]{1,0:T(8,128)S(1)}, f32[1024,128]{1,0:T(8,128)S(1)}, u32[]{:S(2)}, u32[]{:S(2)}) %collective-permute-start.27) | collective-permute-done | bytes 524320 | tf_op jit(solution)/shard_map/ppermute | solution.py:365
  122.6 1.9 collective-permute-start.2
  124.5 8.5 %collective-permute-done.28.refs_3_ = f32[1024,128]{1,0:T(8,128)S(1)} collective-permute-done((f32[1024,128]{1,0:T(8,128)S(1)}, f32[1024,128]{1,0:T(8,128)S(1)}, u32[]{:S(2)}, u32[]{:S(2)}) %collective-permute-start.28) | collective-permute-done | bytes 524320 | tf_op jit(solution)/shard_map/ppermute | solution.py:365
  134.5 5.6 %weight_parts.8 = (f32[2,2,128,512]{3,2,1,0:T(8,128)S(1)}, f32[2,2,128,512]{3,2,1,0:T(8,128)}) custom-call(s32[3]{0:T(128)S(1)} %pad_add_fusion.scal, f32[2,128,1024]{2,1,0:T(8,128)S(1)} %value_grads.4.refs_0_, f32[2,128,1024]{2,1,0:T(8,128)S(1)} %collective-permute-done.12.refs_1_, f32[2,128,1024]{2,1,0:T(8,128)S(1)} %collective-permute-done.13.refs_2_, ...), custom_call_target="tpu_custom_call" | custom-call | flops 3221225472 | bytes 9437184 | tf_op jit(solution)/shard_map/weight_parts/pallas_call | solution.py:267
  140.8 4.0 %value_grads.5 = f32[2,128,1024]{2,1,0:T(8,128)S(1)} custom-call(s32[3]{0:T(128)S(1)} %pad_add_fusion.scal, f32[1024,1024]{1,0:T(8,128)S(1)} %copy-done.2, f32[1024,1024]{1,0:T(8,128)S(1)} %copy-done.9, f32[1024,1024]{1,0:T(8,128)S(1)} %copy-done.6, f32[3,128,128]{2,1,0:T(8,128)S(1)} %get-tuple-element.100.rev.mine, ...), custom_call_target="tpu_custom_call" | custom-call | flops 805306368 | bytes 4194304 | tf_op jit(solution)/shard_map/value_grads/pallas_call | solution.py:122
  144.8 1.7 collective-permute-start.21
  148.9 8.4 %collective-permute-done.18 = f32[2,2,128,512]{3,2,1,0:T(8,128)S(1)} collective-permute-done((f32[2,2,128,512]{3,2,1,0:T(8,128)S(1)}, f32[2,2,128,512]{3,2,1,0:T(8,128)S(1)}, u32[]{:S(2)}, u32[]{:S(2)}) %collective-permute-start.18) | collective-permute-done | bytes 1048608 | tf_op jit(solution)/shard_map/ppermute | solution.py:365
  163.1 1.6 add.102
  164.8 3.8 %collective-permute-done.15 = f32[2,2,128,512]{3,2,1,0:T(8,128)} collective-permute-done((f32[2,2,128,512]{3,2,1,0:T(8,128)}, f32[2,2,128,512]{3,2,1,0:T(8,128)}, u32[]{:S(2)}, u32[]{:S(2)}) %collective-permute-start.15) | collective-permute-done | bytes 1048608 | tf_op jit(solution)/shard_map/ppermute | solution.py:365
  168.7 19.8 %collective-permute-start.19 = (f32[1,2,128,512]{3,2,1,0:T(8,128)S(1)}, f32[1,2,128,512]{3,2,1,0:T(8,128)S(1)}, u32[]{:S(2)}, u32[]{:S(2)}) collective-permute-start(f32[1,2,128,512]{3,2,1,0:T(8,128)S(1)} %slice.125), channel_id=1, source_target_pairs={{0,8},{1,9},{2,10},{3,11},{4,12},{5,13},{6,14},{7,15},{8,0},{9,1},... | collective-permute-start | bytes 1572872 | tf_op jit(solution)/shard_map/ppermute | solution.py:365
  190.8 8.5 %collective-permute-start.16 = (f32[1,2,128,512]{3,2,1,0:T(8,128)S(1)}, f32[1,2,128,512]{3,2,1,0:T(8,128)S(1)}, u32[]{:S(2)}, u32[]{:S(2)}) collective-permute-start(f32[1,2,128,512]{3,2,1,0:T(8,128)S(1)} %slice.121), channel_id=1, source_target_pairs={{0,8},{1,9},{2,10},{3,11},{4,12},{5,13},{6,14},{7,15},{8,0},{9,1},... | collective-permute-start | bytes 1572872 | tf_op jit(solution)/shard_map/ppermute | solution.py:365
  199.5 1.7 collective-permute-start.45
  201.7 7.2 %collective-permute-done.19 = f32[1,2,128,512]{3,2,1,0:T(8,128)S(1)} collective-permute-done((f32[1,2,128,512]{3,2,1,0:T(8,128)S(1)}, f32[1,2,128,512]{3,2,1,0:T(8,128)S(1)}, u32[]{:S(2)}, u32[]{:S(2)}) %collective-permute-start.19) | collective-permute-done | bytes 524320 | tf_op jit(solution)/shard_map/ppermute | solution.py:365
  208.9 2.2 copy-done.12
  211.1 6.1 %query_key_grads.2 = (f32[1024,1024]{1,0:T(8,128)}, f32[1024,1024]{1,0:T(8,128)}) custom-call(s32[3]{0:T(128)S(1)} %pad_add_fusion.scal, f32[1024,1024]{1,0:T(8,128)S(1)} %copy-done.3, f32[1024,1024]{1,0:T(8,128)S(1)} %copy-done.10, f32[1024,1024]{1,0:T(8,128)S(1)} %copy-done.12, f32[1024,1024]{1,0:T(8,128)S(1)} %copy-done.7, ...), custom_call_target="tpu_custom_call" | custom-call | flops 2013265920 | bytes 6291456 | tf_op jit(solution)/shard_map/query_key_grads/pallas_call | solution.py:166
  217.2 2.6 split_terms.5
  221.3 5.1 %collective-permute-done.22.refs_1_ = f32[2,128,1024]{2,1,0:T(8,128)S(1)} collective-permute-done((f32[2,128,1024]{2,1,0:T(8,128)S(1)}, f32[2,128,1024]{2,1,0:T(8,128)S(1)}, u32[]{:S(2)}, u32[]{:S(2)}) %collective-permute-start.22) | collective-permute-done | bytes 1048608 | tf_op jit(solution)/shard_map/ppermute | solution.py:365
  226.4 3.1 collective-permute-start.20
  229.5 6.6 %weight_parts.15 = (f32[2,128,512]{2,1,0:T(8,128)S(1)}, f32[2,128,512]{2,1,0:T(8,128)S(1)}) custom-call(s32[3]{0:T(128)S(1)} %pad_add_fusion.scal, f32[2,128,1024]{2,1,0:T(8,128)} %broadcast_select_fusion.refs_0_, f32[2,128,1024]{2,1,0:T(8,128)} %collective-permute-done.44.refs_1_, f32[2,128,1024]{2,1,0:T(8,128)S(1)} %collective-permute-done.45.refs_2_, ...), custom_call_target="tpu_custom_call" | custom-call | flops 3221225472 | bytes 9437184 | tf_op jit(solution)/shard_map/weight_parts/pallas_call | solution.py:267
  236.0 6.6 %weight_parts.14 = (f32[2,128,512]{2,1,0:T(8,128)S(1)}, f32[2,128,512]{2,1,0:T(8,128)S(1)}) custom-call(s32[3]{0:T(128)S(1)} %pad_add_fusion.scal, f32[2,128,1024]{2,1,0:T(8,128)} %broadcast_select_fusion.refs_0_, f32[2,128,1024]{2,1,0:T(8,128)} %collective-permute-done.44.refs_1_, f32[2,128,1024]{2,1,0:T(8,128)S(1)} %collective-permute-done.45.refs_2_, ...), custom_call_target="tpu_custom_call" | custom-call | flops 3221225472 | bytes 9437184 | tf_op jit(solution)/shard_map/weight_parts/pallas_call | solution.py:267
  244.7 6.6 %weight_parts.13 = (f32[2,128,512]{2,1,0:T(8,128)S(1)}, f32[2,128,512]{2,1,0:T(8,128)S(1)}) custom-call(s32[3]{0:T(128)S(1)} %pad_add_fusion.scal, f32[2,128,1024]{2,1,0:T(8,128)} %broadcast_select_fusion.1.refs_0_, f32[2,128,1024]{2,1,0:T(8,128)} %collective-permute-done.36.refs_1_, f32[2,128,1024]{2,1,0:T(8,128)S(1)} %collective-permute-done.37.refs_2_, ...), custom_call_target="tpu_custom_call" | custom-call | flops 3221225472 | bytes 9437184 | tf_op jit(solution)/shard_map/weight_parts/pallas_call | solution.py:267
  251.3 6.6 %weight_parts.12 = (f32[2,128,512]{2,1,0:T(8,128)S(1)}, f32[2,128,512]{2,1,0:T(8,128)S(1)}) custom-call(s32[3]{0:T(128)S(1)} %pad_add_fusion.scal, f32[2,128,1024]{2,1,0:T(8,128)} %broadcast_select_fusion.1.refs_0_, f32[2,128,1024]{2,1,0:T(8,128)} %collective-permute-done.36.refs_1_, f32[2,128,1024]{2,1,0:T(8,128)S(1)} %collective-permute-done.37.refs_2_, ...), custom_call_target="tpu_custom_call" | custom-call | flops 3221225472 | bytes 9437184 | tf_op jit(solution)/shard_map/weight_parts/pallas_call | solution.py:267
  260.0 4.9 %weight_parts.11 = (f32[2,128,512]{2,1,0:T(8,128)S(1)}, f32[2,128,512]{2,1,0:T(8,128)S(1)}) custom-call(s32[3]{0:T(128)S(1)} %pad_add_fusion.scal, f32[2,128,1024]{2,1,0:T(8,128)S(1)} %broadcast_select_fusion.2.refs_0_, f32[2,128,1024]{2,1,0:T(8,128)S(1)} %collective-permute-done.22.refs_1_, f32[2,128,1024]{2,1,0:T(8,128)S(1)} %collective-permute-done.23.refs_2_, ...), custom_call_target="tpu_custom_call" | custom-call | flops 3221225472 | bytes 9437184 | tf_op jit(solution)/shard_map/weight_parts/pallas_call | solution.py:267
  265.0 5.2 %weight_parts.10 = (f32[2,128,512]{2,1,0:T(8,128)S(1)}, f32[2,128,512]{2,1,0:T(8,128)S(1)}) custom-call(s32[3]{0:T(128)S(1)} %pad_add_fusion.scal, f32[2,128,1024]{2,1,0:T(8,128)S(1)} %broadcast_select_fusion.2.refs_0_, f32[2,128,1024]{2,1,0:T(8,128)S(1)} %collective-permute-done.22.refs_1_, f32[2,128,1024]{2,1,0:T(8,128)S(1)} %collective-permute-done.23.refs_2_, ...), custom_call_target="tpu_custom_call" | custom-call | flops 3221225472 | bytes 9437184 | tf_op jit(solution)/shard_map/weight_parts/pallas_call | solution.py:267
  271.1 8.9 %collective-permute-done.41 = f32[2,128,512]{2,1,0:T(8,128)S(1)} collective-permute-done((f32[2,128,512]{2,1,0:T(8,128)S(1)}, f32[2,128,512]{2,1,0:T(8,128)S(1)}, u32[]{:S(2)}, u32[]{:S(2)}) %collective-permute-start.41) | collective-permute-done | bytes 524320 | tf_op jit(solution)/shard_map/ppermute | solution.py:365
  280.7 10.5 %collective-permute-done.39 = f32[2,128,512]{2,1,0:T(8,128)S(1)} collective-permute-done((f32[2,128,512]{2,1,0:T(8,128)S(1)}, f32[2,128,512]{2,1,0:T(8,128)S(1)}, u32[]{:S(2)}, u32[]{:S(2)}) %collective-permute-start.39) | collective-permute-done | bytes 524320 | tf_op jit(solution)/shard_map/ppermute | solution.py:365
  291.3 11.1 %collective-permute-done.33 = f32[2,128,512]{2,1,0:T(8,128)S(1)} collective-permute-done((f32[2,128,512]{2,1,0:T(8,128)S(1)}, f32[2,128,512]{2,1,0:T(8,128)S(1)}, u32[]{:S(2)}, u32[]{:S(2)}) %collective-permute-start.33) | collective-permute-done | bytes 524320 | tf_op jit(solution)/shard_map/ppermute | solution.py:365
  302.6 10.3 %collective-permute-done.29 = f32[2,128,512]{2,1,0:T(8,128)S(1)} collective-permute-done((f32[2,128,512]{2,1,0:T(8,128)S(1)}, f32[2,128,512]{2,1,0:T(8,128)S(1)}, u32[]{:S(2)}, u32[]{:S(2)}) %collective-permute-start.29) | collective-permute-done | bytes 524320 | tf_op jit(solution)/shard_map/ppermute | solution.py:365
  313.4 2.7 collective-permute-start.40
  316.4 2.6 collective-permute-start.30
  319.0 15.6 %query_key_grads.3 = (f32[1024,1024]{1,0:T(8,128)}, f32[1024,1024]{1,0:T(8,128)}) custom-call(s32[3]{0:T(128)S(1)} %pad_add_fusion.scal, f32[1024,1024]{1,0:T(8,128)S(1)} %copy-done.3, f32[1024,1024]{1,0:T(8,128)S(1)} %copy-done.10, f32[1024,1024]{1,0:T(8,128)S(1)} %copy-done.13, ...), custom_call_target="tpu_custom_call", output_to_operand_aliasing={{0}: (9, {}), {1}: (10, {})} | custom-call | flops 6039797760 | bytes 18874368 | tf_op jit(solution)/shard_map/query_key_grads/pallas_call | solution.py:166
  334.6 2.3 collective-permute-done.40.refs_9_
  336.9 28.1 %collective-permute-done.34.refs_7_ = f32[1,128,512]{2,1,0:T(8,128)S(1)} collective-permute-done((f32[1,128,512]{2,1,0:T(8,128)S(1)}, f32[1,128,512]{2,1,0:T(8,128)S(1)}, u32[]{:S(2)}, u32[]{:S(2)}) %collective-permute-start.34) | collective-permute-done | bytes 262176 | tf_op jit(solution)/shard_map/ppermute | solution.py:365
  365.0 5.5 %collective-permute-done.30.refs_5_ = f32[1,128,512]{2,1,0:T(8,128)S(1)} collective-permute-done((f32[1,128,512]{2,1,0:T(8,128)S(1)}, f32[1,128,512]{2,1,0:T(8,128)S(1)}, u32[]{:S(2)}, u32[]{:S(2)}) %collective-permute-start.30) | collective-permute-done | bytes 262176 | tf_op jit(solution)/shard_map/ppermute | solution.py:365
  370.5 3.1 update_block.1
  (182 shorter events, 32.5 us)
Async XLA Ops:
  6.7 5.3 %collective-permute-start.8 = (f32[1,128,128]{2,1,0:T(8,128)S(1)}, f32[1,128,128]{2,1,0:T(8,128)S(1)}, u32[]{:S(2)}, u32[]{:S(2)}) collective-permute-start(f32[1,128,128]{2,1,0:T(8,128)S(1)} %get-tuple-element.45), channel_id=1, source_target_pairs={{0,4},{1,5},{2,6},{3,7},{4,0},{5,1},{6,2},{7,3},{8,12},{9,13},{10,... | collective-permute-start | bytes 196616 | tf_op jit(solution)/shard_map/ppermute | solution.py:365
  12.0 4.4 %collective-permute-start.9 = (f32[1,128,128]{2,1,0:T(8,128)S(1)}, f32[1,128,128]{2,1,0:T(8,128)S(1)}, u32[]{:S(2)}, u32[]{:S(2)}) collective-permute-start(f32[1,128,128]{2,1,0:T(8,128)S(1)} %add.95), channel_id=1, source_target_pairs={{0,8},{1,9},{2,10},{3,11},{4,12},{5,13},{6,14},{7,15},{8,0},{9,1},... | collective-permute-start | bytes 196616 | tf_op jit(solution)/shard_map/ppermute | solution.py:365
  16.5 7.1 %collective-permute-start.10 = (f32[1,128,128]{2,1,0:T(8,128)S(1)}, f32[1,128,128]{2,1,0:T(8,128)S(1)}, u32[]{:S(2)}, u32[]{:S(2)}) collective-permute-start(f32[1,128,128]{2,1,0:T(8,128)S(1)} %add.96), channel_id=1, source_target_pairs={{16,0},{17,1},{18,2},{19,3},{20,4},{21,5},{22,6},{23,7},{24,8},{25... | collective-permute-start | bytes 196616 | tf_op jit(solution)/shard_map/ppermute | solution.py:365
  23.6 4.3 %collective-permute-start.11 = (f32[1,128,128]{2,1,0:T(8,128)S(1)}, f32[1,128,128]{2,1,0:T(8,128)S(1)}, u32[]{:S(2)}, u32[]{:S(2)}) collective-permute-start(f32[1,128,128]{2,1,0:T(8,128)S(1)} %get-tuple-element.101), channel_id=1, source_target_pairs={{0,4},{1,5},{2,6},{3,7},{4,0},{5,1},{6,2},{7,3},{8,12},{9,13},{10,... | collective-permute-start | bytes 196616 | tf_op jit(solution)/shard_map/ppermute | solution.py:365
  38.5 20.9 %collective-permute-start.12 = (f32[2,128,1024]{2,1,0:T(8,128)S(1)}, f32[2,128,1024]{2,1,0:T(8,128)S(1)}, u32[]{:S(2)}, u32[]{:S(2)}) collective-permute-start(f32[2,128,1024]{2,1,0:T(8,128)S(1)} %value_grads.4.refs_0_), channel_id=1, source_target_pairs={{0,2},{1,3},{2,0},{3,1},{4,6},{5,7},{6,4},{7,5},{8,10},{9,11},{10,... | collective-permute-start | bytes 3145736 | tf_op jit(solution)/shard_map/ppermute | solution.py:365
  44.3 5.7 %collective-permute-start.4 = (f32[3,128,128]{2,1,0:T(8,128)S(1)}, f32[3,128,128]{2,1,0:T(8,128)S(1)}, u32[]{:S(2)}, u32[]{:S(2)}) collective-permute-start(f32[3,128,128]{2,1,0:T(8,128)S(1)} %get-tuple-element.43), channel_id=1, source_target_pairs={{0,4},{1,5},{2,6},{3,7},{4,0},{5,1},{6,2},{7,3},{8,12},{9,13},{10,... | collective-permute-start | bytes 589832 | tf_op jit(solution)/shard_map/ppermute | solution.py:365
  50.0 9.4 %collective-permute-start.5 = (f32[3,128,128]{2,1,0:T(8,128)S(1)}, f32[3,128,128]{2,1,0:T(8,128)S(1)}, u32[]{:S(2)}, u32[]{:S(2)}) collective-permute-start(f32[3,128,128]{2,1,0:T(8,128)S(1)} %add.90), channel_id=1, source_target_pairs={{0,8},{1,9},{2,10},{3,11},{4,12},{5,13},{6,14},{7,15},{8,0},{9,1},... | collective-permute-start | bytes 589832 | tf_op jit(solution)/shard_map/ppermute | solution.py:365
  51.7 43.3 %collective-permute-start.13 = (f32[2,128,1024]{2,1,0:T(8,128)S(1)}, f32[2,128,1024]{2,1,0:T(8,128)S(1)}, u32[]{:S(2)}, u32[]{:S(2)}) collective-permute-start(f32[2,128,1024]{2,1,0:T(8,128)S(1)} %value_grads.4.refs_0_), channel_id=1, source_target_pairs={{0,1},{1,0},{2,3},{3,2},{4,5},{5,4},{6,7},{7,6},{8,9},{9,8},{10,11... | collective-permute-start | bytes 3145736 | tf_op jit(solution)/shard_map/ppermute | solution.py:365
  51.8 22.1 %collective-permute-start.25 = (f32[1024,128]{1,0:T(8,128)S(1)}, f32[1024,128]{1,0:T(8,128)S(1)}, u32[]{:S(2)}, u32[]{:S(2)}) collective-permute-start(f32[1024,128]{1,0:T(8,128)S(1)} %get-tuple-element.80), channel_id=1, source_target_pairs={{0,8},{1,9},{2,10},{3,11},{4,12},{5,13},{6,14},{7,15},{8,0},{9,1},... | collective-permute-start | bytes 1572872 | tf_op jit(solution)/shard_map/ppermute | solution.py:365
  57.1 37.9 %copy-start.15 = (f32[4,128,128]{2,1,0:T(8,128)}, f32[4,128,128]{2,1,0:T(8,128)S(1)}, u32[]{:S(2)}) copy-start(f32[4,128,128]{2,1,0:T(8,128)S(1)} %get-tuple-element.40) | copy-start | bytes 786436
  57.1 8.5 %collective-permute-start = (f32[4,128,128]{2,1,0:T(8,128)S(1)}, f32[4,128,128]{2,1,0:T(8,128)S(1)}, u32[]{:S(2)}, u32[]{:S(2)}) collective-permute-start(f32[4,128,128]{2,1,0:T(8,128)S(1)} %get-tuple-element.41), channel_id=1, source_target_pairs={{0,4},{1,5},{2,6},{3,7},{4,0},{5,1},{6,2},{7,3},{8,12},{9,13},{10,... | collective-permute-start | bytes 786440 | tf_op jit(solution)/shard_map/ppermute | solution.py:365
  59.4 41.4 %collective-permute-start.14 = (f32[2,128,1024]{2,1,0:T(8,128)S(1)}, f32[2,128,1024]{2,1,0:T(8,128)S(1)}, u32[]{:S(2)}, u32[]{:S(2)}) collective-permute-start(f32[2,128,1024]{2,1,0:T(8,128)S(1)} %collective-permute-done.12.refs_1_), channel_id=1, source_target_pairs={{0,1},{1,0},{2,3},{3,2},{4,5},{5,4},{6,7},{7,6},{8,9},{9,8},{10,11... | collective-permute-start | bytes 3145736 | tf_op jit(solution)/shard_map/ppermute | solution.py:365
  59.4 14.5 %collective-permute-start.6 = (f32[3,128,128]{2,1,0:T(8,128)S(1)}, f32[3,128,128]{2,1,0:T(8,128)S(1)}, u32[]{:S(2)}, u32[]{:S(2)}) collective-permute-start(f32[3,128,128]{2,1,0:T(8,128)S(1)} %add.91), channel_id=1, source_target_pairs={{16,0},{17,1},{18,2},{19,3},{20,4},{21,5},{22,6},{23,7},{24,8},{25... | collective-permute-start | bytes 589832 | tf_op jit(solution)/shard_map/ppermute | solution.py:365
  65.6 17.7 %collective-permute-start.26 = (f32[1024,128]{1,0:T(8,128)S(1)}, f32[1024,128]{1,0:T(8,128)S(1)}, u32[]{:S(2)}, u32[]{:S(2)}) collective-permute-start(f32[1024,128]{1,0:T(8,128)S(1)} %get-tuple-element.79), channel_id=1, source_target_pairs={{0,8},{1,9},{2,10},{3,11},{4,12},{5,13},{6,14},{7,15},{8,0},{9,1},... | collective-permute-start | bytes 1572872 | tf_op jit(solution)/shard_map/ppermute | solution.py:365
  73.9 15.0 %collective-permute-start.1 = (f32[4,128,128]{2,1,0:T(8,128)S(1)}, f32[4,128,128]{2,1,0:T(8,128)S(1)}, u32[]{:S(2)}, u32[]{:S(2)}) collective-permute-start(f32[4,128,128]{2,1,0:T(8,128)S(1)} %add.85), channel_id=1, source_target_pairs={{0,8},{1,9},{2,10},{3,11},{4,12},{5,13},{6,14},{7,15},{8,0},{9,1},... | collective-permute-start | bytes 786440 | tf_op jit(solution)/shard_map/ppermute | solution.py:365
  74.0 15.0 %collective-permute-start.7 = (f32[3,128,128]{2,1,0:T(8,128)S(1)}, f32[3,128,128]{2,1,0:T(8,128)S(1)}, u32[]{:S(2)}, u32[]{:S(2)}) collective-permute-start(f32[3,128,128]{2,1,0:T(8,128)S(1)} %get-tuple-element.99), channel_id=1, source_target_pairs={{0,4},{1,5},{2,6},{3,7},{4,0},{5,1},{6,2},{7,3},{8,12},{9,13},{10,... | collective-permute-start | bytes 589832 | tf_op jit(solution)/shard_map/ppermute | solution.py:365
  83.3 57.5 %collective-permute-start.31 = (f32[1024,256]{1,0:T(8,128)S(1)}, f32[1024,256]{1,0:T(8,128)S(1)}, u32[]{:S(2)}, u32[]{:S(2)}) collective-permute-start(f32[1024,256]{1,0:T(8,128)S(1)} %get-tuple-element.76), channel_id=1, source_target_pairs={{0,8},{1,9},{2,10},{3,11},{4,12},{5,13},{6,14},{7,15},{8,0},{9,1},... | collective-permute-start | bytes 3145736 | tf_op jit(solution)/shard_map/ppermute | solution.py:365
  88.9 33.7 %collective-permute-start.27 = (f32[1024,128]{1,0:T(8,128)S(1)}, f32[1024,128]{1,0:T(8,128)S(1)}, u32[]{:S(2)}, u32[]{:S(2)}) collective-permute-start(f32[1024,128]{1,0:T(8,128)S(1)} %get-tuple-element.78), channel_id=1, source_target_pairs={{0,8},{1,9},{2,10},{3,11},{4,12},{5,13},{6,14},{7,15},{8,0},{9,1},... | collective-permute-start | bytes 1572872 | tf_op jit(solution)/shard_map/ppermute | solution.py:365
  88.9 44.1 %collective-permute-start.28 = (f32[1024,128]{1,0:T(8,128)S(1)}, f32[1024,128]{1,0:T(8,128)S(1)}, u32[]{:S(2)}, u32[]{:S(2)}) collective-permute-start(f32[1024,128]{1,0:T(8,128)S(1)} %get-tuple-element.77), channel_id=1, source_target_pairs={{0,8},{1,9},{2,10},{3,11},{4,12},{5,13},{6,14},{7,15},{8,0},{9,1},... | collective-permute-start | bytes 1572872 | tf_op jit(solution)/shard_map/ppermute | solution.py:365
  95.0 49.8 %collective-permute-start.43 = (f32[2,128,1024]{2,1,0:T(8,128)S(1)}, f32[2,128,1024]{2,1,0:T(8,128)S(1)}, u32[]{:S(2)}, u32[]{:S(2)}) collective-permute-start(f32[2,128,1024]{2,1,0:T(8,128)S(1)} %value_grads.7), channel_id=1, source_target_pairs={{1,8},{3,10},{5,12},{7,14},{8,1},{10,3},{12,5},{14,7},{17,24},{19,... | collective-permute-start | bytes 3145736 | tf_op jit(solution)/shard_map/ppermute | solution.py:365
  96.7 37.8 %copy-start.33 = (bf16[4,1024,256]{2,1,0:T(8,128)(2,1)}, bf16[4,1024,256]{2,1,0:T(8,128)(2,1)S(1)}, u32[]{:S(2)}) copy-start(bf16[4,1024,256]{2,1,0:T(8,128)(2,1)S(1)} %get-tuple-element.50.refs_4_) | copy-start | bytes 6291460
  96.7 37.8 %copy-start.35 = (bf16[4,1024,256]{2,1,0:T(8,128)(2,1)}, bf16[4,1024,256]{2,1,0:T(8,128)(2,1)S(1)}, u32[]{:S(2)}) copy-start(bf16[4,1024,256]{2,1,0:T(8,128)(2,1)S(1)} %get-tuple-element.51.refs_5_) | copy-start | bytes 6291460
  100.8 46.9 %collective-permute-start.35 = (f32[2,128,1024]{2,1,0:T(8,128)S(1)}, f32[2,128,1024]{2,1,0:T(8,128)S(1)}, u32[]{:S(2)}, u32[]{:S(2)}) collective-permute-start(f32[2,128,1024]{2,1,0:T(8,128)S(1)} %value_grads.6), channel_id=1, source_target_pairs={{1,8},{3,10},{5,12},{7,14},{8,1},{10,3},{12,5},{14,7},{17,24},{19,... | collective-permute-start | bytes 3145736 | tf_op jit(solution)/shard_map/ppermute | solution.py:365
  122.6 17.5 %collective-permute-start.2 = (f32[4,128,128]{2,1,0:T(8,128)S(1)}, f32[4,128,128]{2,1,0:T(8,128)S(1)}, u32[]{:S(2)}, u32[]{:S(2)}) collective-permute-start(f32[4,128,128]{2,1,0:T(8,128)S(1)} %add.86), channel_id=1, source_target_pairs={{0,16},{1,17},{2,18},{3,19},{4,20},{5,21},{6,22},{7,23},{8,24},{9,... | collective-permute-start | bytes 786440 | tf_op jit(solution)/shard_map/ppermute | solution.py:365
  133.0 24.3 %collective-permute-start.18 = (f32[2,2,128,512]{3,2,1,0:T(8,128)S(1)}, f32[2,2,128,512]{3,2,1,0:T(8,128)S(1)}, u32[]{:S(2)}, u32[]{:S(2)}) collective-permute-start(f32[2,2,128,512]{3,2,1,0:T(8,128)S(1)} %get-tuple-element.55), channel_id=1, source_target_pairs={{0,4},{1,5},{2,6},{3,7},{4,0},{5,1},{6,2},{7,3},{8,12},{9,13},{10,... | collective-permute-start | bytes 3145736 | tf_op jit(solution)/shard_map/ppermute | solution.py:365
  140.2 28.5 %collective-permute-start.15 = (f32[2,2,128,512]{3,2,1,0:T(8,128)}, f32[2,2,128,512]{3,2,1,0:T(8,128)}, u32[]{:S(2)}, u32[]{:S(2)}) collective-permute-start(f32[2,2,128,512]{3,2,1,0:T(8,128)} %get-tuple-element.53), channel_id=1, source_target_pairs={{0,4},{1,5},{2,6},{3,7},{4,0},{5,1},{6,2},{7,3},{8,12},{9,13},{10,... | collective-permute-start | bytes 3145736 | tf_op jit(solution)/shard_map/ppermute | solution.py:365
  140.8 49.4 %collective-permute-start.32 = (f32[1024,256]{1,0:T(8,128)}, f32[1024,256]{1,0:T(8,128)}, u32[]{:S(2)}, u32[]{:S(2)}) collective-permute-start(f32[1024,256]{1,0:T(8,128)} %get-tuple-element.75), channel_id=1, source_target_pairs={{0,8},{1,9},{2,10},{3,11},{4,12},{5,13},{6,14},{7,15},{8,0},{9,1},... | collective-permute-start | bytes 3145736 | tf_op jit(solution)/shard_map/ppermute | solution.py:365
  144.8 46.0 %collective-permute-start.21 = (f32[2,128,1024]{2,1,0:T(8,128)S(1)}, f32[2,128,1024]{2,1,0:T(8,128)}, u32[]{:S(2)}, u32[]{:S(2)}) collective-permute-start(f32[2,128,1024]{2,1,0:T(8,128)S(1)} %value_grads.5), channel_id=1, source_target_pairs={{1,8},{3,10},{5,12},{7,14},{8,1},{10,3},{12,5},{14,7},{17,24},{19,... | collective-permute-start | bytes 3145736 | tf_op jit(solution)/shard_map/ppermute | solution.py:365
  147.7 53.6 %collective-permute-start.44 = (f32[2,128,1024]{2,1,0:T(8,128)}, f32[2,128,1024]{2,1,0:T(8,128)}, u32[]{:S(2)}, u32[]{:S(2)}) collective-permute-start(f32[2,128,1024]{2,1,0:T(8,128)} %broadcast_select_fusion.refs_0_), channel_id=1, source_target_pairs={{0,2},{1,3},{2,0},{3,1},{4,6},{5,7},{6,4},{7,5},{8,10},{9,11},{10,... | collective-permute-start | bytes 3145736 | tf_op jit(solution)/shard_map/ppermute | solution.py:365
  158.3 61.7 %collective-permute-start.36 = (f32[2,128,1024]{2,1,0:T(8,128)}, f32[2,128,1024]{2,1,0:T(8,128)}, u32[]{:S(2)}, u32[]{:S(2)}) collective-permute-start(f32[2,128,1024]{2,1,0:T(8,128)} %broadcast_select_fusion.1.refs_0_), channel_id=1, source_target_pairs={{0,2},{1,3},{2,0},{3,1},{4,6},{5,7},{6,4},{7,5},{8,10},{9,11},{10,... | collective-permute-start | bytes 3145736 | tf_op jit(solution)/shard_map/ppermute | solution.py:365
  162.5 26.0 %copy-start.41 = (f32[4,128,128]{2,1,0:T(8,128)S(1)}, f32[4,128,128]{2,1,0:T(8,128)}, u32[]{:S(2)}) copy-start(f32[4,128,128]{2,1,0:T(8,128)} %copy-done.40) | copy-start | bytes 786436
  162.5 26.0 %copy-start.43 = (f32[4,128,128]{2,1,0:T(8,128)S(1)}, f32[4,128,128]{2,1,0:T(8,128)}, u32[]{:S(2)}) copy-start(f32[4,128,128]{2,1,0:T(8,128)} %copy-done.42) | copy-start | bytes 786436
  163.1 45.8 %copy-start.10 = (f32[1024,1024]{1,0:T(8,128)S(1)}, f32[1024,1024]{1,0:T(8,128)}, u32[]{:S(2)}) copy-start(f32[1024,1024]{1,0:T(8,128)} %k.11) | copy-start | bytes 12582916
  164.8 44.1 %copy-start.3 = (f32[1024,1024]{1,0:T(8,128)S(1)}, f32[1024,1024]{1,0:T(8,128)}, u32[]{:S(2)}) copy-start(f32[1024,1024]{1,0:T(8,128)} %q.11) | copy-start | bytes 12582916
  164.8 44.1 %copy-start.7 = (f32[1024,1024]{1,0:T(8,128)S(1)}, f32[1024,1024]{1,0:T(8,128)}, u32[]{:S(2)}) copy-start(f32[1024,1024]{1,0:T(8,128)} %g.11) | copy-start | bytes 12582916
  164.8 44.1 %copy-start.20 = (f32[1,128,128]{2,1,0:T(8,128)S(1)}, f32[1,128,128]{2,1,0:T(8,128)}, u32[]{:S(2)}) copy-start(f32[1,128,128]{2,1,0:T(8,128)} %copy-done.19) | copy-start | bytes 196612
  164.8 44.1 %copy-start.30 = (f32[1,128,128]{2,1,0:T(8,128)S(1)}, f32[1,128,128]{2,1,0:T(8,128)}, u32[]{:S(2)}) copy-start(f32[1,128,128]{2,1,0:T(8,128)} %copy-done.29) | copy-start | bytes 196612
  168.7 40.2 %collective-permute-start.19 = (f32[1,2,128,512]{3,2,1,0:T(8,128)S(1)}, f32[1,2,128,512]{3,2,1,0:T(8,128)S(1)}, u32[]{:S(2)}, u32[]{:S(2)}) collective-permute-start(f32[1,2,128,512]{3,2,1,0:T(8,128)S(1)} %slice.125), channel_id=1, source_target_pairs={{0,8},{1,9},{2,10},{3,11},{4,12},{5,13},{6,14},{7,15},{8,0},{9,1},... | collective-permute-start | bytes 1572872 | tf_op jit(solution)/shard_map/ppermute | solution.py:365
  190.2 9.4 %collective-permute-start.3 = (f32[4,128,128]{2,1,0:T(8,128)S(1)}, f32[4,128,128]{2,1,0:T(8,128)S(1)}, u32[]{:S(2)}, u32[]{:S(2)}) collective-permute-start(f32[4,128,128]{2,1,0:T(8,128)S(1)} %get-tuple-element.97), channel_id=1, source_target_pairs={{0,4},{1,5},{2,6},{3,7},{4,0},{5,1},{6,2},{7,3},{8,12},{9,13},{10,... | collective-permute-start | bytes 786440 | tf_op jit(solution)/shard_map/ppermute | solution.py:365
  190.8 29.8 %collective-permute-start.16 = (f32[1,2,128,512]{3,2,1,0:T(8,128)S(1)}, f32[1,2,128,512]{3,2,1,0:T(8,128)S(1)}, u32[]{:S(2)}, u32[]{:S(2)}) collective-permute-start(f32[1,2,128,512]{3,2,1,0:T(8,128)S(1)} %slice.121), channel_id=1, source_target_pairs={{0,8},{1,9},{2,10},{3,11},{4,12},{5,13},{6,14},{7,15},{8,0},{9,1},... | collective-permute-start | bytes 1572872 | tf_op jit(solution)/shard_map/ppermute | solution.py:365
  199.5 21.2 %collective-permute-start.45 = (f32[2,128,1024]{2,1,0:T(8,128)}, f32[2,128,1024]{2,1,0:T(8,128)S(1)}, u32[]{:S(2)}, u32[]{:S(2)}) collective-permute-start(f32[2,128,1024]{2,1,0:T(8,128)} %broadcast_select_fusion.refs_0_), channel_id=1, source_target_pairs={{0,1},{1,0},{2,3},{3,2},{4,5},{5,4},{6,7},{7,6},{8,9},{9,8},{10,11... | collective-permute-start | bytes 3145736 | tf_op jit(solution)/shard_map/ppermute | solution.py:365
  201.2 25.1 %collective-permute-start.22 = (f32[2,128,1024]{2,1,0:T(8,128)S(1)}, f32[2,128,1024]{2,1,0:T(8,128)S(1)}, u32[]{:S(2)}, u32[]{:S(2)}) collective-permute-start(f32[2,128,1024]{2,1,0:T(8,128)S(1)} %broadcast_select_fusion.2.refs_0_), channel_id=1, source_target_pairs={{0,2},{1,3},{2,0},{3,1},{4,6},{5,7},{6,4},{7,5},{8,10},{9,11},{10,... | collective-permute-start | bytes 3145736 | tf_op jit(solution)/shard_map/ppermute | solution.py:365
  208.9 17.5 %collective-permute-start.46 = (f32[2,128,1024]{2,1,0:T(8,128)}, f32[2,128,1024]{2,1,0:T(8,128)S(1)}, u32[]{:S(2)}, u32[]{:S(2)}) collective-permute-start(f32[2,128,1024]{2,1,0:T(8,128)} %collective-permute-done.44.refs_1_), channel_id=1, source_target_pairs={{0,1},{1,0},{2,3},{3,2},{4,5},{5,4},{6,7},{7,6},{8,9},{9,8},{10,11... | collective-permute-start | bytes 3145736 | tf_op jit(solution)/shard_map/ppermute | solution.py:365
  220.0 22.7 %collective-permute-start.37 = (f32[2,128,1024]{2,1,0:T(8,128)}, f32[2,128,1024]{2,1,0:T(8,128)S(1)}, u32[]{:S(2)}, u32[]{:S(2)}) collective-permute-start(f32[2,128,1024]{2,1,0:T(8,128)} %broadcast_select_fusion.1.refs_0_), channel_id=1, source_target_pairs={{0,1},{1,0},{2,3},{3,2},{4,5},{5,4},{6,7},{7,6},{8,9},{9,8},{10,11... | collective-permute-start | bytes 3145736 | tf_op jit(solution)/shard_map/ppermute | solution.py:365
  220.5 22.7 %collective-permute-start.38 = (f32[2,128,1024]{2,1,0:T(8,128)}, f32[2,128,1024]{2,1,0:T(8,128)S(1)}, u32[]{:S(2)}, u32[]{:S(2)}) collective-permute-start(f32[2,128,1024]{2,1,0:T(8,128)} %collective-permute-done.36.refs_1_), channel_id=1, source_target_pairs={{0,1},{1,0},{2,3},{3,2},{4,5},{5,4},{6,7},{7,6},{8,9},{9,8},{10,11... | collective-permute-start | bytes 3145736 | tf_op jit(solution)/shard_map/ppermute | solution.py:365
  220.8 37.1 %collective-permute-start.23 = (f32[2,128,1024]{2,1,0:T(8,128)S(1)}, f32[2,128,1024]{2,1,0:T(8,128)S(1)}, u32[]{:S(2)}, u32[]{:S(2)}) collective-permute-start(f32[2,128,1024]{2,1,0:T(8,128)S(1)} %broadcast_select_fusion.2.refs_0_), channel_id=1, source_target_pairs={{0,1},{1,0},{2,3},{3,2},{4,5},{5,4},{6,7},{7,6},{8,9},{9,8},{10,11... | collective-permute-start | bytes 3145736 | tf_op jit(solution)/shard_map/ppermute | solution.py:365
  226.4 32.1 %collective-permute-start.24 = (f32[2,128,1024]{2,1,0:T(8,128)S(1)}, f32[2,128,1024]{2,1,0:T(8,128)S(1)}, u32[]{:S(2)}, u32[]{:S(2)}) collective-permute-start(f32[2,128,1024]{2,1,0:T(8,128)S(1)} %collective-permute-done.22.refs_1_), channel_id=1, source_target_pairs={{0,1},{1,0},{2,3},{3,2},{4,5},{5,4},{6,7},{7,6},{8,9},{9,8},{10,11... | collective-permute-start | bytes 3145736 | tf_op jit(solution)/shard_map/ppermute | solution.py:365
  226.4 87.0 %collective-permute-start.20 = (f32[1,128,512]{2,1,0:T(8,128)S(1)}, f32[1,128,512]{2,1,0:T(8,128)S(1)}, u32[]{:S(2)}, u32[]{:S(2)}) collective-permute-start(f32[1,128,512]{2,1,0:T(8,128)S(1)} %get-tuple-element.93), channel_id=1, source_target_pairs={{0,16},{1,17},{2,18},{3,19},{4,20},{5,21},{6,22},{7,23},{8,24},{9,... | collective-permute-start | bytes 786440 | tf_op jit(solution)/shard_map/ppermute | solution.py:365
  242.6 27.5 %collective-permute-start.49 = (f32[2,128,512]{2,1,0:T(8,128)S(1)}, f32[2,128,512]{2,1,0:T(8,128)S(1)}, u32[]{:S(2)}, u32[]{:S(2)}) collective-permute-start(f32[2,128,512]{2,1,0:T(8,128)S(1)} %get-tuple-element.71), channel_id=1, source_target_pairs={{0,4},{1,5},{2,6},{3,7},{4,0},{5,1},{6,2},{7,3},{8,12},{9,13},{10,... | collective-permute-start | bytes 1572872 | tf_op jit(solution)/shard_map/ppermute | solution.py:365
  243.2 27.6 %collective-permute-start.47 = (f32[2,128,512]{2,1,0:T(8,128)S(1)}, f32[2,128,512]{2,1,0:T(8,128)S(1)}, u32[]{:S(2)}, u32[]{:S(2)}) collective-permute-start(f32[2,128,512]{2,1,0:T(8,128)S(1)} %get-tuple-element.69), channel_id=1, source_target_pairs={{0,4},{1,5},{2,6},{3,7},{4,0},{5,1},{6,2},{7,3},{8,12},{9,13},{10,... | collective-permute-start | bytes 1572872 | tf_op jit(solution)/shard_map/ppermute | solution.py:365
  257.9 22.1 %collective-permute-start.41 = (f32[2,128,512]{2,1,0:T(8,128)S(1)}, f32[2,128,512]{2,1,0:T(8,128)S(1)}, u32[]{:S(2)}, u32[]{:S(2)}) collective-permute-start(f32[2,128,512]{2,1,0:T(8,128)S(1)} %get-tuple-element.67), channel_id=1, source_target_pairs={{0,4},{1,5},{2,6},{3,7},{4,0},{5,1},{6,2},{7,3},{8,12},{9,13},{10,... | collective-permute-start | bytes 1572872 | tf_op jit(solution)/shard_map/ppermute | solution.py:365
  258.5 32.7 %collective-permute-start.39 = (f32[2,128,512]{2,1,0:T(8,128)S(1)}, f32[2,128,512]{2,1,0:T(8,128)S(1)}, u32[]{:S(2)}, u32[]{:S(2)}) collective-permute-start(f32[2,128,512]{2,1,0:T(8,128)S(1)} %get-tuple-element.65), channel_id=1, source_target_pairs={{0,4},{1,5},{2,6},{3,7},{4,0},{5,1},{6,2},{7,3},{8,12},{9,13},{10,... | collective-permute-start | bytes 1572872 | tf_op jit(solution)/shard_map/ppermute | solution.py:365
  270.1 32.3 %collective-permute-start.33 = (f32[2,128,512]{2,1,0:T(8,128)S(1)}, f32[2,128,512]{2,1,0:T(8,128)S(1)}, u32[]{:S(2)}, u32[]{:S(2)}) collective-permute-start(f32[2,128,512]{2,1,0:T(8,128)S(1)} %get-tuple-element.63), channel_id=1, source_target_pairs={{0,4},{1,5},{2,6},{3,7},{4,0},{5,1},{6,2},{7,3},{8,12},{9,13},{10,... | collective-permute-start | bytes 1572872 | tf_op jit(solution)/shard_map/ppermute | solution.py:365
  270.9 45.2 %collective-permute-start.17 = (f32[1,128,512]{2,1,0:T(8,128)S(1)}, f32[1,128,512]{2,1,0:T(8,128)S(1)}, u32[]{:S(2)}, u32[]{:S(2)}) collective-permute-start(f32[1,128,512]{2,1,0:T(8,128)S(1)} %get-tuple-element.95), channel_id=1, source_target_pairs={{0,16},{1,17},{2,18},{3,19},{4,20},{5,21},{6,22},{7,23},{8,24},{9,... | collective-permute-start | bytes 786440 | tf_op jit(solution)/shard_map/ppermute | solution.py:365
  280.0 33.0 %collective-permute-start.29 = (f32[2,128,512]{2,1,0:T(8,128)S(1)}, f32[2,128,512]{2,1,0:T(8,128)S(1)}, u32[]{:S(2)}, u32[]{:S(2)}) collective-permute-start(f32[2,128,512]{2,1,0:T(8,128)S(1)} %get-tuple-element.59), channel_id=1, source_target_pairs={{0,4},{1,5},{2,6},{3,7},{4,0},{5,1},{6,2},{7,3},{8,12},{9,13},{10,... | collective-permute-start | bytes 1572872 | tf_op jit(solution)/shard_map/ppermute | solution.py:365
  280.7 38.3 %copy-start.13 = (f32[1024,1024]{1,0:T(8,128)S(1)}, f32[1024,1024]{1,0:T(8,128)}, u32[]{:S(2)}) copy-start(f32[1024,1024]{1,0:T(8,128)} %v.3) | copy-start | bytes 12582916
  291.2 25.2 %collective-permute-start.50 = (f32[1,128,512]{2,1,0:T(8,128)S(1)}, f32[1,128,512]{2,1,0:T(8,128)S(1)}, u32[]{:S(2)}, u32[]{:S(2)}) collective-permute-start(f32[1,128,512]{2,1,0:T(8,128)S(1)} %get-tuple-element.81), channel_id=1, source_target_pairs={{0,16},{1,17},{2,18},{3,19},{4,20},{5,21},{6,22},{7,23},{8,24},{9,... | collective-permute-start | bytes 786440 | tf_op jit(solution)/shard_map/ppermute | solution.py:365
  302.4 32.1 %collective-permute-start.48 = (f32[1,128,512]{2,1,0:T(8,128)S(1)}, f32[1,128,512]{2,1,0:T(8,128)S(1)}, u32[]{:S(2)}, u32[]{:S(2)}) collective-permute-start(f32[1,128,512]{2,1,0:T(8,128)S(1)} %get-tuple-element.83), channel_id=1, source_target_pairs={{0,16},{1,17},{2,18},{3,19},{4,20},{5,21},{6,22},{7,23},{8,24},{9,... | collective-permute-start | bytes 786440 | tf_op jit(solution)/shard_map/ppermute | solution.py:365
  312.9 21.6 %collective-permute-start.42 = (f32[1,128,512]{2,1,0:T(8,128)S(1)}, f32[1,128,512]{2,1,0:T(8,128)S(1)}, u32[]{:S(2)}, u32[]{:S(2)}) collective-permute-start(f32[1,128,512]{2,1,0:T(8,128)S(1)} %get-tuple-element.85), channel_id=1, source_target_pairs={{0,16},{1,17},{2,18},{3,19},{4,20},{5,21},{6,22},{7,23},{8,24},{9,... | collective-permute-start | bytes 786440 | tf_op jit(solution)/shard_map/ppermute | solution.py:365
  313.4 23.5 %collective-permute-start.40 = (f32[1,128,512]{2,1,0:T(8,128)S(1)}, f32[1,128,512]{2,1,0:T(8,128)S(1)}, u32[]{:S(2)}, u32[]{:S(2)}) collective-permute-start(f32[1,128,512]{2,1,0:T(8,128)S(1)} %get-tuple-element.87), channel_id=1, source_target_pairs={{0,16},{1,17},{2,18},{3,19},{4,20},{5,21},{6,22},{7,23},{8,24},{9,... | collective-permute-start | bytes 786440 | tf_op jit(solution)/shard_map/ppermute | solution.py:365
  316.1 48.9 %collective-permute-start.34 = (f32[1,128,512]{2,1,0:T(8,128)S(1)}, f32[1,128,512]{2,1,0:T(8,128)S(1)}, u32[]{:S(2)}, u32[]{:S(2)}) collective-permute-start(f32[1,128,512]{2,1,0:T(8,128)S(1)} %get-tuple-element.89), channel_id=1, source_target_pairs={{0,16},{1,17},{2,18},{3,19},{4,20},{5,21},{6,22},{7,23},{8,24},{9,... | collective-permute-start | bytes 786440 | tf_op jit(solution)/shard_map/ppermute | solution.py:365
  316.4 54.1 %collective-permute-start.30 = (f32[1,128,512]{2,1,0:T(8,128)S(1)}, f32[1,128,512]{2,1,0:T(8,128)S(1)}, u32[]{:S(2)}, u32[]{:S(2)}) collective-permute-start(f32[1,128,512]{2,1,0:T(8,128)S(1)} %get-tuple-element.91), channel_id=1, source_target_pairs={{0,16},{1,17},{2,18},{3,19},{4,20},{5,21},{6,22},{7,23},{8,24},{9,... | collective-permute-start | bytes 786440 | tf_op jit(solution)/shard_map/ppermute | solution.py:365
  319.0 51.5 %copy-start.31 = (f32[1,1024]{1,0:T(1,128)S(1)}, f32[1,1024]{1,0:T(1,128)}, u32[]{:S(2)}) copy-start(f32[1,1024]{1,0:T(1,128)} %col_state.1) | copy-start | bytes 12292
  319.0 51.5 %copy-start.32 = (f32[1,512]{1,0:T(1,128)S(1)}, f32[1,512]{1,0:T(1,128)}, u32[]{:S(2)}) copy-start(f32[1,512]{1,0:T(1,128)} %row_state.1) | copy-start | bytes 6148
  (31 other events, 263.0 us)
